TPU v7x, 128 devices: a whole 4x4x4 slice. The times are simulated.
128 devices in a mesh: head: 16 (over y_lo, z, core), blk: 8 (over x, y_hi).
Axes of the slice: x: 4, y: 4 (y_hi: 2, y_lo: 2; y = y_hi * 2 + y_lo), z: 4, core: 2. Of those that a mesh axis runs over, the one named last changes fastest.
Arguments:
- query_head_matrix: bfloat16 [16384, 8192], P(('blk', 'head')), may hold values from -8 to 8
- key_matrix: bfloat16 [16384, 1024], P(('blk', 'head')), may hold values from -8 to 8
- value_matrix: bfloat16 [16384, 1024], P(('blk', 'head')), may hold values from -6 to 6
- output_gradient: bfloat16 [16384, 8192], P(('blk', 'head')), may hold values from -6 to 6
- span_lengths: int32 [62], replicated, may hold values from 1 to 512, 15872 in all
Outputs:
- attended: bfloat16 [16384, 8192], P(('blk', 'head'))
- query_grad: bfloat16 [16384, 8192], P(('blk', 'head'))
- key_gradient: bfloat16 [16384, 1024], P(('blk', 'head'))
- value_gradient: bfloat16 [16384, 1024], P(('blk', 'head'))
Inputs may be any that keep to these rules, and one draw needn't show every extreme that they name: `span_lengths`: the 62 span lengths sum to 15872, and the longest span holds exactly 512 tokens.
All inputs are finite; a program needn't handle non-finite values.
Results may differ from a plain program's by a relative error of at most 0.02.
Values may be sent and summed in bfloat16 or wider, within the bound.
No kernel may reach another device: no remote copies, remote signals or barrier semaphores. Data moves between devices by JAX's collectives and lax.ppermute only.
A program may use at most 128 MiB of HBM per device.

v0:
```python
import math

import jax
import jax.numpy as jnp
from jax import lax
from jax.experimental import pallas as pl
from jax.experimental.pallas import tpu as pltpu
from jax.sharding import Mesh
from jax.sharding import PartitionSpec as P


QUERY_HEADS = 64
KEY_VALUE_HEADS = 8
HEAD_WIDTH = 128
GROUP = QUERY_HEADS // KEY_VALUE_HEADS
QLEN = 512
ROWS = 128
BACK = 4
SPANS = 62
AXES = ("x", "yh", "yl", "z", "c")
MESH_AXES = ("yl", "z", "c", "x", "yh")
PLANE = ("x", "yh", "yl")
DEVICES = 128
CONTEXT = DEVICES * ROWS - QLEN
RING = 8 * ROWS
SCALE = 1.0 / math.sqrt(HEAD_WIDTH)
SCALE2 = SCALE * math.log2(math.e)
HIDDEN = -1e30
FLOOR = -1e29
BF16 = jnp.bfloat16
F32 = jnp.float32


HUBS = ((0, 3), (2, 3), (3, 0), (3, 2))
QUADRANTS = (
    ((0, 0), (0, 1), (0, 2), (0, 3)),
    ((2, 0), (2, 1), (2, 2), (2, 3)),
    ((3, 0), (3, 1), (1, 0), (1, 1)),
    ((3, 2), (3, 3), (1, 2), (1, 3)),
)


def dot_nt(a, b):
    return lax.dot_general(a, b, (((1,), (1,)), ((), ())), preferred_element_type=F32)


def dot_nn(a, b):
    return lax.dot_general(a, b, (((1,), (0,)), ((), ())), preferred_element_type=F32)


def stacked(pair):
    return jnp.concatenate([pair[:, :HEAD_WIDTH], pair[:, HEAD_WIDTH:]], axis=0)


def unstacked(transposed):
    rows = transposed.T
    return jnp.concatenate([rows[:ROWS], rows[ROWS:]], axis=1).astype(BF16)


def context_kernel(
    place_ref, span_ref, q_ref, g_ref, same0, same1, same2, swapped0, swapped1, swapped2, *rest,
):
    rest = rest[-14:]
    out_ref, dq_ref, d0, d1, d2, d3, d4, bias, k_win, v_win, k_t, v_t, dk_acc, dv_acc = rest
    window = (BACK + 1) * ROWS
    group, pair = pl.program_id(0), pl.program_id(1)
    place = place_ref[0]

    @pl.when((group == 0) & (pair == 0))
    def _():
        row = place * ROWS + lax.broadcasted_iota(jnp.int32, (1, ROWS), 1)

        def step(n, carry):
            begin, start = carry
            start = jnp.where(row >= begin, begin, start)
            return begin + span_ref[n], start

        _, start = lax.fori_loop(0, SPANS, step, (jnp.int32(0), jnp.zeros((1, ROWS), jnp.int32)))
        start = jnp.where(row >= CONTEXT, DEVICES * ROWS, start)
        key = (place - BACK) * ROWS + lax.broadcasted_iota(jnp.int32, (window, ROWS), 0)
        bias[...] = jnp.where((key >= start) & (key <= row), 0.0, HIDDEN)

    def fill(i, ref):
        k_win[i * ROWS : (i + 1) * ROWS] = ref[0, 0]
        v_win[i * ROWS : (i + 1) * ROWS] = ref[0, 1]
        k_t[:, i * ROWS : (i + 1) * ROWS] = ref[0, 0].T
        v_t[:, i * ROWS : (i + 1) * ROWS] = ref[0, 1].T

    @pl.when(pair == 0)
    def _():
        fill(0, same2)
        fill(2, same1)
        fill(4, same0)
        dk_acc[...] = jnp.zeros_like(dk_acc)
        dv_acc[...] = jnp.zeros_like(dv_acc)

    @pl.when((pair == 0) & (place % 2 == 0))
    def _():
        fill(1, swapped2)
        fill(3, swapped1)

    @pl.when((pair == 0) & (place % 2 == 1))
    def _():
        fill(1, swapped1)
        fill(3, swapped0)

    q = stacked(q_ref[...])
    g = stacked(g_ref[...])
    hide = jnp.concatenate([bias[...], bias[...]], axis=1)
    s = dot_nt(k_win[...], q) * SCALE2 + hide
    top = jnp.maximum(jnp.max(s, axis=0, keepdims=True), FLOOR)
    w = jnp.exp2(s - top)
    total = jnp.sum(w, axis=0, keepdims=True)
    p = w * jnp.where(total > 0.0, 1.0 / total, 0.0)
    dp = dot_nt(v_win[...], g)
    dd = jnp.sum(p * dp, axis=0, keepdims=True)
    ds = (p * (dp - dd)).astype(BF16)
    pb = p.astype(BF16)
    out_ref[...] = unstacked(dot_nn(v_t[...], pb))
    dq_ref[...] = unstacked(dot_nn(k_t[...], ds) * SCALE)
    dv_acc[...] += dot_nn(pb, g)
    dk_acc[...] += dot_nn(ds, q)

    @pl.when(pair == GROUP // 2 - 1)
    def _():
        for i, ref in enumerate((d4, d3, d2, d1, d0)):
            ref[0, 0] = (dk_acc[i * ROWS : (i + 1) * ROWS] * SCALE).astype(BF16)
            ref[0, 1] = dv_acc[i * ROWS : (i + 1) * ROWS].astype(BF16)


def context_attention(first, count, place, span_lengths, q, g, blocks, before=()):
    window = (BACK + 1) * ROWS
    wide = pl.BlockSpec((ROWS, 2 * HEAD_WIDTH), lambda a, b, *_: (0, (a + first) * (GROUP // 2) + b))
    block = pl.BlockSpec((1, 2, ROWS, HEAD_WIDTH), lambda a, b, *_: (a + first, 0, 0, 0))
    whole = jax.ShapeDtypeStruct(q.shape, BF16)
    part = jax.ShapeDtypeStruct((KEY_VALUE_HEADS, 2, ROWS, HEAD_WIDTH), BF16)
    return pl.pallas_call(
        context_kernel,
        grid_spec=pltpu.PrefetchScalarGridSpec(
            num_scalar_prefetch=2,
            grid=(count, GROUP // 2),
            in_specs=[wide, wide] + [block] * 6 + [pl.BlockSpec(memory_space=pl.ANY)] * len(before),
            out_specs=[wide, wide] + [block] * 5,
            scratch_shapes=[
                pltpu.VMEM((window, ROWS), F32),
                pltpu.VMEM((window, HEAD_WIDTH), BF16),
                pltpu.VMEM((window, HEAD_WIDTH), BF16),
                pltpu.VMEM((HEAD_WIDTH, window), BF16),
                pltpu.VMEM((HEAD_WIDTH, window), BF16),
                pltpu.VMEM((window, HEAD_WIDTH), F32),
                pltpu.VMEM((window, HEAD_WIDTH), F32),
            ],
        ),
        out_shape=[whole, whole] + [part] * 5,
        input_output_aliases={10 + i: i for i in range(len(before))},
        name="context_rows",
    )(place, span_lengths, q, g, *blocks, *before)


def question_scores(place_ref, ring, k, q):
    s = dot_nt(k, q) * SCALE2
    lane = lax.broadcasted_iota(jnp.int32, (1, 2 * ROWS), 1) % ROWS
    x, y = lane // 32, lane // 8 % 4
    piece = jnp.where(x % 2 == 0, x * 2 + y, 8 + y // 2 * 4 + y % 2 + (3 - x))
    row = CONTEXT + place_ref[0] // 32 * ROWS + piece * 8 + lane % 8
    key = ring_of(place_ref[0], ring) * RING + lax.broadcasted_iota(jnp.int32, s.shape, 0)
    return jnp.where(key <= row, s, HIDDEN)


def ring_of(place, ring):
    return (place // 32 + 4 - ring) % 4 * 4 + place // 8 % 4


def question_pair(qg_ref, which):
    return stacked(qg_ref[:, which].reshape(ROWS, 2 * HEAD_WIDTH))


def ring_keys(kv_ref):
    return kv_ref[0, :, 0].reshape(RING, HEAD_WIDTH), kv_ref[0, :, 1].reshape(RING, HEAD_WIDTH)


def statistics_kernel(place_ref, qg_ref, kv_ref, stats_ref):
    pair, ring = pl.program_id(0), pl.program_id(1)
    k, v = ring_keys(kv_ref)
    q = question_pair(qg_ref, 0)
    g = question_pair(qg_ref, 1)
    s = question_scores(place_ref, ring, k, q)
    slots = [pl.ds(pl.multiple_of(part * GROUP, GROUP) + pair, 1) for part in range(3)]

    @pl.when(ring == 0)
    def _():
        stats_ref[slots[0], :] = jnp.full((1, 2 * ROWS), FLOOR, F32)
        stats_ref[slots[1], :] = jnp.zeros((1, 2 * ROWS), F32)
        stats_ref[slots[2], :] = jnp.zeros((1, 2 * ROWS), F32)

    before = stats_ref[slots[0], :]
    top = jnp.maximum(before, jnp.max(s, axis=0, keepdims=True))
    factor = jnp.exp2(before - top)
    w = jnp.exp2(s - top)
    stats_ref[slots[0], :] = top
    stats_ref[slots[1], :] = stats_ref[slots[1], :] * factor + jnp.sum(w, axis=0, keepdims=True)
    dd = jnp.sum(w * dot_nt(v, g), axis=0, keepdims=True)
    stats_ref[slots[2], :] = stats_ref[slots[2], :] * factor + dd


def question_kernel(
    place_ref, qg_ref, kv_ref, stats_ref, part_ref, dkv_ref, k_t, v_t, dk_acc, dv_acc, out_acc, dq_acc
):
    ring, pair = pl.program_id(0), pl.program_id(1)
    k, v = ring_keys(kv_ref)

    @pl.when(pair == 0)
    def _():
        k_t[...] = k.T
        v_t[...] = v.T
        dk_acc[...] = jnp.zeros_like(dk_acc)
        dv_acc[...] = jnp.zeros_like(dv_acc)

    @pl.when(ring == 0)
    def _():
        out_acc[pair] = jnp.zeros((HEAD_WIDTH, 2 * ROWS), F32)
        dq_acc[pair] = jnp.zeros((HEAD_WIDTH, 2 * ROWS), F32)

    q = question_pair(qg_ref, 0)
    g = question_pair(qg_ref, 1)
    s = question_scores(place_ref, ring, k, q)
    lse = stats_ref[pl.ds(pair, 1), :]
    dd = stats_ref[pl.ds(GROUP + pair, 1), :]
    p = jnp.exp2(s - lse)
    ds = (p * (dot_nt(v, g) - dd)).astype(BF16)
    pb = p.astype(BF16)
    out_acc[pair] += dot_nn(v_t[...], pb)
    dq_acc[pair] += dot_nn(k_t[...], ds)
    dv_acc[...] += dot_nn(pb, g)
    dk_acc[...] += dot_nn(ds, q)

    @pl.when(ring == 3)
    def _():
        shape = (16, 8, 2 * HEAD_WIDTH)
        part_ref[:, 0] = unstacked(out_acc[pair]).reshape(shape)
        part_ref[:, 1] = unstacked(dq_acc[pair] * SCALE).reshape(shape)

    @pl.when(pair == GROUP // 2 - 1)
    def _():
        dkv_ref[0, :, 0] = (dk_acc[...] * SCALE).astype(BF16).reshape(8, ROWS, HEAD_WIDTH)
        dkv_ref[0, :, 1] = dv_acc[...].astype(BF16).reshape(8, ROWS, HEAD_WIDTH)


def question_statistics(place, qg, kv):
    return pl.pallas_call(
        statistics_kernel,
        grid_spec=pltpu.PrefetchScalarGridSpec(
            num_scalar_prefetch=1,
            grid=(GROUP // 2, 4),
            in_specs=[
                pl.BlockSpec((16, 2, 8, 2 * HEAD_WIDTH), lambda h, r, *_: (0, 0, 0, h)),
                pl.BlockSpec((1, 8, 2, ROWS, HEAD_WIDTH), lambda h, r, *_: (r, 0, 0, 0, 0)),
            ],
            out_specs=pl.BlockSpec((3 * GROUP, 2 * ROWS), lambda h, r, *_: (0, 0)),
        ),
        out_shape=jax.ShapeDtypeStruct((3 * GROUP, 2 * ROWS), F32),
        name="question_statistics",
    )(place, qg, kv)


def question_attention(place, qg, kv, stats):
    rows = pl.BlockSpec((16, 2, 8, 2 * HEAD_WIDTH), lambda r, h, *_: (0, 0, 0, h))
    keys = pl.BlockSpec((1, 8, 2, ROWS, HEAD_WIDTH), lambda r, h, *_: (r, 0, 0, 0, 0))
    last_rows = pl.BlockSpec(
        (16, 2, 8, 2 * HEAD_WIDTH), lambda r, h, *_: (0, 0, 0, jnp.where(r == 3, h, 0))
    )
    return pl.pallas_call(
        question_kernel,
        grid_spec=pltpu.PrefetchScalarGridSpec(
            num_scalar_prefetch=1,
            grid=(4, GROUP // 2),
            in_specs=[rows, keys, pl.BlockSpec((2 * GROUP, 2 * ROWS), lambda r, h, *_: (0, 0))],
            out_specs=[last_rows, keys],
            scratch_shapes=[
                pltpu.VMEM((HEAD_WIDTH, RING), BF16),
                pltpu.VMEM((HEAD_WIDTH, RING), BF16),
                pltpu.VMEM((RING, HEAD_WIDTH), F32),
                pltpu.VMEM((RING, HEAD_WIDTH), F32),
                pltpu.VMEM((GROUP // 2, HEAD_WIDTH, 2 * ROWS), F32),
                pltpu.VMEM((GROUP // 2, HEAD_WIDTH, 2 * ROWS), F32),
            ],
        ),
        out_shape=[
            jax.ShapeDtypeStruct(qg.shape, BF16),
            jax.ShapeDtypeStruct(kv.shape, BF16),
        ],
        name="question_rows",
    )(place, qg, kv, stats)


def copied(sources, targets, done):
    for pairs in (sources, targets):
        copies = [pltpu.make_async_copy(a, b, done.at[i]) for i, (a, b) in enumerate(pairs)]
        for copy in copies:
            copy.start()
        for copy in copies:
            copy.wait()


def move_call(kernel, place, arrays, shapes, room, copies, aliases=None):
    anywhere = pl.BlockSpec(memory_space=pl.ANY)
    return pl.pallas_call(
        kernel,
        grid_spec=pltpu.PrefetchScalarGridSpec(
            num_scalar_prefetch=1,
            grid=(1,),
            in_specs=[anywhere] * len(arrays),
            out_specs=[anywhere] * len(shapes),
            scratch_shapes=[pltpu.VMEM(room, BF16), pltpu.SemaphoreType.DMA((copies,))],
        ),
        out_shape=[jax.ShapeDtypeStruct(shape, BF16) for shape in shapes],
        input_output_aliases=aliases or {},
    )(place, *arrays)


def pieces_kernel(place_ref, q_ref, g_ref, p0, p1, p2, p3, room, done):
    @pl.when(place_ref[0] >= CONTEXT // ROWS)
    def _():
        targets = []
        for j, piece in enumerate((p0, p1, p2, p3)):
            for t in range(4):
                for which in range(2):
                    rows = pl.ds(32 * j + 8 * t, 8)
                    targets.append((room.at[which, rows], piece.at[t, which]))
        copied([(q_ref, room.at[0]), (g_ref, room.at[1])], targets, done)


def question_pieces(place, q, g):
    width = q.shape[1]
    return move_call(pieces_kernel, place, (q, g), [(4, 2, 8, width)] * 4, (2, ROWS, width), 32)


def spokes_kernel(place_ref, p0, p1, p2, p3, s0, s1, s2, s3, room, done):
    ring = place_ref[0] // 8
    for hub, piece, members in zip(HUBS, (p0, p1, p2, p3), QUADRANTS):

        @pl.when((ring == hub[0] * 4 + hub[1]) & (place_ref[0] % 8 >= 4))
        def _():
            first = members.index(hub)
            targets = [(room.at[(first + d) % 4], s) for d, s in enumerate((s0, s1, s2, s3))]
            copied([(piece, room)], targets, done)


def question_spokes(place, pieces):
    shape = pieces[0].shape
    return move_call(spokes_kernel, place, pieces, [shape[1:]] * 4, shape, 4)


def pick_kernel(place_ref, s0, s1, s2, s3, deal_ref, room, done):
    x, y = place_ref[0] // 32, place_ref[0] // 8 % 4
    step = jnp.where(x % 2 == 0, (y + 1) % 4, y % 2 + 3 - x)
    wide = GROUP * HEAD_WIDTH
    for d, piece in enumerate((s0, s1, s2, s3)):

        @pl.when((step == d) & (place_ref[0] % 8 >= 4))
        def _():
            groups = range(KEY_VALUE_HEADS)
            targets = [(room.at[:, :, pl.ds(k * wide, wide)], deal_ref.at[k]) for k in groups]
            copied([(piece, room)], targets, done)


def question_pick(place, spokes):
    shape = spokes[0].shape
    deal = (KEY_VALUE_HEADS, 2, 8, GROUP * HEAD_WIDTH)
    return move_call(pick_kernel, place, spokes, [deal], shape, KEY_VALUE_HEADS)[0]


def results_kernel(place_ref, out_in, dq_in, b0, b1, b2, b3, out_ref, dq_ref, room, done):
    @pl.when(place_ref[0] >= CONTEXT // ROWS)
    def _():
        sources, targets = [], []
        for j, back in enumerate((b0, b1, b2, b3)):
            sources.append((back, room.at[j]))
            for t in range(4):
                for which, ref in enumerate((out_ref, dq_ref)):
                    rows = pl.ds(32 * j + 8 * t, 8)
                    targets.append((room.at[j, t, which], ref.at[rows]))
        copied(sources, targets, done)


def question_results(place, out, dq, back):
    return move_call(
        results_kernel, place, (out, dq, *back), [out.shape] * 2,
        (4,) + back[0].shape, 32, {1: 0, 2: 1},
    )


def permuted(block, pairs):
    index = [place % 16 * 8 + place // 16 for place in range(DEVICES)]
    return lax.ppermute(block, MESH_AXES, [(index[i], index[j]) for i, j in pairs])


def shifted(block, distance):
    pairs = [(i, i + distance) for i in range(CONTEXT // ROWS)]
    return permuted(block, [(i, j) for i, j in pairs if 0 <= j < CONTEXT // ROWS])


def swapped(block):
    return permuted(block, [(i, i ^ 1) for i in range(DEVICES)])


def turned(block, distance):
    return permuted(block, [(i, (i + 32 * distance) % DEVICES) for i in range(DEVICES)])


def in_ring(ring, holder):
    return (ring[0] * 4 + ring[1]) * 8 + 4 + holder


def hub_pairs(j):
    return [(DEVICES - 4 + o, in_ring(HUBS[j], o)) for o in range(4)]


def spoke_pairs(d):
    pairs = []
    for hub, members in zip(HUBS, QUADRANTS):
        member = members[(members.index(hub) + d) % 4]
        pairs += [(in_ring(hub, o), in_ring(member, o)) for o in range(4)]
    return pairs


def back_to_front(pairs):
    return [(j, i) for i, j in pairs]


def exchanged(blocks, axes):
    return lax.all_to_all(blocks, axes, split_axis=0, concat_axis=0, tiled=True)


def merged(stats):
    parts = exchanged(jnp.broadcast_to(stats, (4,) + stats.shape), ("yh", "yl"))
    tops, totals, sums = jnp.split(parts, 3, axis=1)
    top = jnp.max(tops, axis=0)
    factor = jnp.exp2(tops - top)
    total = jnp.sum(totals * factor, axis=0)
    return jnp.concatenate([top + jnp.log2(total), jnp.sum(sums * factor, axis=0) / total])


def added(*terms):
    return sum(t.astype(F32) for t in terms)


def shards(q, k, v, g, span_lengths):
    place = lax.axis_index(AXES)
    place_arg = place.reshape(1).astype(jnp.int32)
    even = place % 2 == 0
    even_x = place // 32 % 2 == 0
    wide = GROUP * HEAD_WIDTH
    barrier = lax.optimization_barrier

    def headed(a):
        return a.reshape(ROWS, KEY_VALUE_HEADS, HEAD_WIDTH).transpose(1, 0, 2)

    kv = jnp.stack([headed(k), headed(v)], axis=1)
    kv_ring = exchanged(kv, ("z", "c"))
    pieces = question_pieces(place_arg, q, g)
    pieces = [permuted(pieces[j], hub_pairs(j)) for j in range(4)]
    same1 = shifted(kv, 2)
    same2 = shifted(same1, 2)
    blocks = (kv, same1, same2, swapped(kv), swapped(same1), swapped(same2))

    pieces, blocks = barrier((pieces, blocks))
    spokes = question_spokes(place_arg, pieces)
    spokes = [spokes[0]] + [permuted(spokes[d], spoke_pairs(d)) for d in (1, 2, 3)]
    context = context_attention(0, 2, place_arg, span_lengths, q, g, blocks)
    spokes, kv_ring, context = barrier((spokes, kv_ring, context))
    kv_ring = [kv_ring] + [turned(kv_ring, i) for i in (1, 2, 3)]
    deal = exchanged(question_pick(place_arg, spokes), ("z", "c"))
    context = context_attention(2, 2, place_arg, span_lengths, q, g, blocks, context)
    deal, context = barrier((deal, context))
    own = jnp.broadcast_to(deal[4:, None], (4, 4, 2, 8, wide))
    qg = exchanged(own.reshape(16, 2, 8, wide), PLANE)
    context = context_attention(4, 2, place_arg, span_lengths, q, g, blocks, context)
    qg, kv_ring, context = barrier((qg, jnp.stack(kv_ring), context))

    stats = question_statistics(place_arg, qg, kv_ring)
    stats, context = barrier((stats, context))
    context = context_attention(6, 2, place_arg, span_lengths, q, g, blocks, context)
    stats, context = barrier((merged(stats), context))
    parts, dkv_ring = question_attention(place_arg, qg, kv_ring, stats)
    parts, dkv_ring, context = barrier((parts, dkv_ring, context))
    out, dq, d0, d1, d2, d3, d4 = context
    from1, from3 = swapped(d1), swapped(d3)
    none = jnp.zeros_like(d1)
    far = shifted(added(d4, jnp.where(even, none, from3)).astype(BF16), -2)
    near = shifted(added(d2, jnp.where(even, from3, from1), far).astype(BF16), -2)

    parts = exchanged(parts, PLANE)
    parts = jnp.sum(parts.reshape(4, 4, 2, 8, wide).astype(F32), axis=1).astype(BF16)
    parts = exchanged(jnp.concatenate([jnp.zeros_like(parts), parts]), ("z", "c"))
    parts, dkv_ring = barrier((parts, dkv_ring))
    mine = parts.transpose(1, 2, 0, 3).reshape(2, 8, KEY_VALUE_HEADS * wide)
    gathered = [permuted(mine, back_to_front(spoke_pairs(d))) for d in (1, 2, 3)]
    hub = jnp.where(even_x, jnp.stack(gathered + [mine]), jnp.stack([mine] + gathered))
    back = [permuted(hub, back_to_front(hub_pairs(j))) for j in range(4)]

    turns = [turned(dkv_ring[i], -i) for i in (1, 2, 3)]
    dkv_ring = added(dkv_ring[0], *turns)
    dkv_ring = exchanged(dkv_ring.astype(BF16), ("z", "c"))
    dkv = added(d0, jnp.where(even, from1, none), near, dkv_ring).astype(BF16)
    dk = dkv[:, 0].transpose(1, 0, 2).reshape(k.shape)
    dv = dkv[:, 1].transpose(1, 0, 2).reshape(v.shape)

    out, dq = question_results(place_arg, out, dq, back)
    return out, dq, dk, dv


def solution(mesh):
    grid = Mesh(mesh.devices.reshape(2, 4, 2, 4, 2), MESH_AXES)
    rows = P(AXES, None)
    return jax.shard_map(
        shards,
        mesh=grid,
        in_specs=(rows, rows, rows, rows, P()),
        out_specs=(rows,) * 4,
        check_vma=False,
    )
```

profile of v0, /device:TPU:1, one launch (start us, length us, event | category | flops | bytes accessed | tf_op | source)
XLA Modules:
  0.0 268.1 jit_solution(3781448096087037716)
XLA Ops:
  4.1 4.4 %collective-permute-start.4 = (bf16[8,2,128,128]{3,2,1,0:T(8,128)(2,1)}, bf16[8,2,128,128]{3,2,1,0:T(8,128)(2,1)S(1)}, u32[]{:S(2)}, u32[]{:S(2)}) collective-permute-start(bf16[8,2,128,128]{3,2,1,0:T(8,128)(2,1)} %pad_maximum_fusion.1.same0), channel_id=1, source_target_pairs={{0,16},{8,24},{16,32},{24,40},{32,48},{40,56},{48,64},{56,72},{64,... | collective-permute-start | bytes 1572872 | tf_op jit(solution)/shard_map/ppermute | solution.py:395
  10.6 1.7 collective-permute-start.1
  13.9 5.5 %collective-permute-done.4.same1 = bf16[8,2,128,128]{3,2,1,0:T(8,128)(2,1)S(1)} collective-permute-done((bf16[8,2,128,128]{3,2,1,0:T(8,128)(2,1)}, bf16[8,2,128,128]{3,2,1,0:T(8,128)(2,1)S(1)}, u32[]{:S(2)}, u32[]{:S(2)}) %collective-permute-start.4) | collective-permute-done | bytes 524320 | tf_op jit(solution)/shard_map/ppermute | solution.py:395
  21.0 4.0 %collective-permute-start.5 = (bf16[8,2,128,128]{3,2,1,0:T(8,128)(2,1)S(1)}, bf16[8,2,128,128]{3,2,1,0:T(8,128)(2,1)S(1)}, u32[]{:S(2)}, u32[]{:S(2)}) collective-permute-start(bf16[8,2,128,128]{3,2,1,0:T(8,128)(2,1)S(1)} %collective-permute-done.4.same1), channel_id=1, source_target_pairs={{0,16},{8,24},{16,32},{24,40},{32,48},{40,56},{48,64},{56,72},{64,... | collective-permute-start | bytes 1572872 | tf_op jit(solution)/shard_map/ppermute | solution.py:395
  25.1 1.9 collective-permute-start.7
  27.0 7.8 %collective-permute-done.5.same2 = bf16[8,2,128,128]{3,2,1,0:T(8,128)(2,1)S(1)} collective-permute-done((bf16[8,2,128,128]{3,2,1,0:T(8,128)(2,1)S(1)}, bf16[8,2,128,128]{3,2,1,0:T(8,128)(2,1)S(1)}, u32[]{:S(2)}, u32[]{:S(2)}) %collective-permute-start.5) | collective-permute-done | bytes 524320 | tf_op jit(solution)/shard_map/ppermute | solution.py:395
  34.7 2.4 collective-permute-start.8
  37.1 6.0 %all-to-all-start = ((bf16[8,2,128,128]{3,2,1,0:T(8,128)(2,1)}), bf16[8,2,128,128]{3,2,1,0:T(8,128)(2,1)S(1)}, u32[]{:S(2)}, u32[]{:S(2)}) async-start(bf16[8,2,128,128]{3,2,1,0:T(8,128)(2,1)} %pad_maximum_fusion.1.same0), calls=%async_computation | async-start | bytes 1048576 | tf_op jit(solution)/shard_map/all_to_all | solution.py:432
  46.2 12.7 %context_rows.4 = (bf16[128,8192]{1,0:T(8,128)(2,1)}, bf16[128,8192]{1,0:T(8,128)(2,1)}, bf16[8,2,128,128]{3,2,1,0:T(8,128)(2,1)}, bf16[8,2,128,128]{3,2,1,0:T(8...) custom-call(s32[1]{0:T(128)} %bitcast.place_ref, ...), custom_call_target="tpu_custom_call" | custom-call | tf_op jit(solution)/shard_map/context_rows/pallas_call | solution.py:137
  59.8 7.4 %all-to-all-start.1 = ((bf16[8,2,8,1024]{3,2,1,0:T(8,128)(2,1)}), bf16[8,2,8,1024]{3,2,1,0:T(8,128)(2,1)S(1)}, u32[]{:S(2)}, u32[]{:S(2)}) async-start(bf16[8,2,8,1024]{3,2,1,0:T(8,128)(2,1)} %shard_map.86), calls=%async_computation.1 | async-start | bytes 524288 | tf_op jit(solution)/shard_map/all_to_all | solution.py:432
  67.2 19.2 %collective-permute-start.14 = (bf16[8,2,128,128]{3,2,1,0:T(8,128)(2,1)S(1)}, bf16[8,2,128,128]{3,2,1,0:T(8,128)(2,1)S(1)}, u32[]{:S(2)}, u32[]{:S(2)}) collective-permute-start(bf16[8,2,128,128]{3,2,1,0:T(8,128)(2,1)S(1)} %all-to-all-done), channel_id=1, source_target_pairs={{0,6},{8,14},{16,22},{24,30},{32,38},{40,46},{48,54},{56,62},{64,7... | collective-permute-start | bytes 1572872 | tf_op jit(solution)/shard_map/ppermute | solution.py:395
  87.0 12.7 %context_rows.5 = (bf16[128,8192]{1,0:T(8,128)(2,1)}, bf16[128,8192]{1,0:T(8,128)(2,1)}, bf16[8,2,128,128]{3,2,1,0:T(8,128)(2,1)}, bf16[8,2,128,128]{3,2,1,0:T(8...) custom-call(s32[1]{0:T(128)} %bitcast.place_ref, ...), custom_call_target="tpu_custom_call", output_to_operand_aliasing={{0}: (10, {}), {1}: (11, {}), {2}: (12, {}), {3}: (13, {}),... | custom-call | tf_op jit(solution)/shard_map/context_rows/pallas_call | solution.py:137
  100.6 5.2 %all-to-all-start.2 = ((bf16[16,2,8,1024]{3,2,1,0:T(8,128)(2,1)}), bf16[16,2,8,1024]{3,2,1,0:T(8,128)(2,1)S(1)}, u32[]{:S(2)}, u32[]{:S(2)}) async-start(bf16[16,2,8,1024]{3,2,1,0:T(8,128)(2,1)} %bitcast.7), calls=%async_computation.2 | async-start | bytes 1048576 | tf_op jit(solution)/shard_map/all_to_all | solution.py:432
  105.8 12.7 %context_rows.6 = (bf16[128,8192]{1,0:T(8,128)(2,1)}, bf16[128,8192]{1,0:T(8,128)(2,1)}, bf16[8,2,128,128]{3,2,1,0:T(8,128)(2,1)}, bf16[8,2,128,128]{3,2,1,0:T(8...) custom-call(s32[1]{0:T(128)} %bitcast.place_ref, ...), custom_call_target="tpu_custom_call", output_to_operand_aliasing={{0}: (10, {}), {1}: (11, {}), {2}: (12, {}), {3}: (13, {}),... | custom-call | tf_op jit(solution)/shard_map/context_rows/pallas_call | solution.py:137
  121.0 17.4 %question_statistics.1 = f32[24,256]{1,0:T(8,128)} custom-call(s32[1]{0:T(128)} %bitcast.place_ref, bf16[16,2,8,1024]{3,2,1,0:T(8,128)(2,1)} %copy-done.10, bf16[4,8,2,128,128]{4,3,2,1,0:T(8,128)(2,1)} %pad_maximum_fusion.kv_ref), custom_call_target="tpu_custom_call" | custom-call | tf_op jit(solution)/shard_map/question_statistics/pallas_call | solution.py:250
  139.7 4.1 %all-to-all-start.3 = ((f32[4,24,256]{2,1,0:T(8,128)}), f32[4,24,256]{2,1,0:T(8,128)S(1)}, u32[]{:S(2)}, u32[]{:S(2)}) async-start(f32[4,24,256]{2,1,0:T(8,128)} %broadcast_in_dim.7), calls=%async_computation.3 | async-start | bytes 196608 | tf_op jit(solution)/shard_map/all_to_all | solution.py:432
  143.8 12.7 %context_rows.7 = (bf16[128,8192]{1,0:T(8,128)(2,1)}, bf16[128,8192]{1,0:T(8,128)(2,1)}, bf16[8,2,128,128]{3,2,1,0:T(8,128)(2,1)}, bf16[8,2,128,128]{3,2,1,0:T(8...) custom-call(s32[1]{0:T(128)} %bitcast.place_ref, ...), custom_call_target="tpu_custom_call", output_to_operand_aliasing={{0}: (10, {}), {1}: (11, {}), {2}: (12, {}), {3}: (13, {}),... | custom-call | tf_op jit(solution)/shard_map/context_rows/pallas_call | solution.py:137
  157.2 20.7 %question_rows.1 = (bf16[16,2,8,1024]{3,2,1,0:T(8,128)(2,1)}, bf16[4,8,2,128,128]{4,3,2,1,0:T(8,128)(2,1)}) custom-call(s32[1]{0:T(128)} %bitcast.place_ref, bf16[16,2,8,1024]{3,2,1,0:T(8,128)(2,1)} %copy-done.10, bf16[4,8,2,128,128]{4,3,2,1,0:T(8,128)(2,1)} %pad_maximum_fusion.kv_ref, f32[16,256]{1,0:T(8,128)} %pad_maximum_fusion.2.stats_ref), custom_call_target="tpu_custom_call" | custom-call | tf_op jit(solution)/shard_map/question_rows/pallas_call | solution.py:272
  177.9 6.8 %all-to-all-start.4 = ((bf16[16,2,8,1024]{3,2,1,0:T(8,128)(2,1)}), bf16[16,2,8,1024]{3,2,1,0:T(8,128)(2,1)S(1)}, u32[]{:S(2)}, u32[]{:S(2)}) async-start(bf16[16,2,8,1024]{3,2,1,0:T(8,128)(2,1)} %get-tuple-element.205), calls=%async_computation.4 | async-start | bytes 1048576 | tf_op jit(solution)/shard_map/all_to_all | solution.py:432
  184.7 2.3 collective-permute-start.23
  187.1 6.7 %all-to-all-done.4 = bf16[16,2,8,1024]{3,2,1,0:T(8,128)(2,1)S(1)} async-done(((bf16[16,2,8,1024]{3,2,1,0:T(8,128)(2,1)}), bf16[16,2,8,1024]{3,2,1,0:T(8,128)(2,1)S(1)}, u32[]{:S(2)}, u32[]{:S(2)}) %all-to-all-start.4) | async-done | bytes 524320 | tf_op jit(solution)/shard_map/all_to_all | solution.py:432
  194.7 7.9 %all-to-all-start.5 = ((bf16[8,2,8,1024]{3,2,1,0:T(8,128)(2,1)}), bf16[8,2,8,1024]{3,2,1,0:T(8,128)(2,1)S(1)}, u32[]{:S(2)}, u32[]{:S(2)}) async-start(bf16[8,2,8,1024]{3,2,1,0:T(8,128)(2,1)} %concatenate.7), calls=%async_computation.5 | async-start | bytes 524288 | tf_op jit(solution)/shard_map/all_to_all | solution.py:432
  202.6 2.2 add_convert_fusion.2
  206.1 3.0 %all-to-all-done.5 = bf16[8,2,8,1024]{3,2,1,0:T(8,128)(2,1)S(1)} async-done(((bf16[8,2,8,1024]{3,2,1,0:T(8,128)(2,1)}), bf16[8,2,8,1024]{3,2,1,0:T(8,128)(2,1)S(1)}, u32[]{:S(2)}, u32[]{:S(2)}) %all-to-all-start.5) | async-done | bytes 262176 | tf_op jit(solution)/shard_map/all_to_all | solution.py:432
  216.7 1.7 collective-permute-start.18
  218.4 1.8 collective-permute-done.24
  221.8 2.2 add_convert_fusion.1
  226.8 10.3 %collective-permute-done.27 = bf16[8,2,128,128]{3,2,1,0:T(8,128)(2,1)S(1)} collective-permute-done((bf16[8,2,128,128]{3,2,1,0:T(8,128)(2,1)S(1)}, bf16[8,2,128,128]{3,2,1,0:T(8,128)(2,1)S(1)}, u32[]{:S(2)}, u32[]{:S(2)}) %collective-permute-start.27) | collective-permute-done | bytes 524320 | tf_op jit(solution)/shard_map/ppermute | solution.py:395
  238.8 6.2 %collective-permute-done.26 = bf16[8,2,128,128]{3,2,1,0:T(8,128)(2,1)S(1)} collective-permute-done((bf16[8,2,128,128]{3,2,1,0:T(8,128)(2,1)S(1)}, bf16[8,2,128,128]{3,2,1,0:T(8,128)(2,1)S(1)}, u32[]{:S(2)}, u32[]{:S(2)}) %collective-permute-start.26) | collective-permute-done | bytes 524320 | tf_op jit(solution)/shard_map/ppermute | solution.py:395
  247.4 7.3 %all-to-all-start.6 = ((bf16[8,2,128,128]{3,2,1,0:T(8,128)(2,1)}), bf16[8,2,128,128]{3,2,1,0:T(8,128)(2,1)S(1)}, u32[]{:S(2)}, u32[]{:S(2)}) async-start(bf16[8,2,128,128]{3,2,1,0:T(8,128)(2,1)} %fusion.2), calls=%async_computation.6 | async-start | bytes 1048576 | tf_op jit(solution)/shard_map/all_to_all | solution.py:432
  254.7 5.6 %collective-permute-done.25 = bf16[8,2,128,128]{3,2,1,0:T(8,128)(2,1)} collective-permute-done((bf16[8,2,128,128]{3,2,1,0:T(8,128)(2,1)}, bf16[8,2,128,128]{3,2,1,0:T(8,128)(2,1)}, u32[]{:S(2)}, u32[]{:S(2)}) %collective-permute-start.25) | collective-permute-done | bytes 524320 | tf_op jit(solution)/shard_map/ppermute | solution.py:395
  260.3 3.8 %all-to-all-done.6 = bf16[8,2,128,128]{3,2,1,0:T(8,128)(2,1)S(1)} async-done(((bf16[8,2,128,128]{3,2,1,0:T(8,128)(2,1)}), bf16[8,2,128,128]{3,2,1,0:T(8,128)(2,1)S(1)}, u32[]{:S(2)}, u32[]{:S(2)}) %all-to-all-start.6) | async-done | bytes 524320 | tf_op jit(solution)/shard_map/all_to_all | solution.py:432
  (109 shorter events, 40.7 us)
Async XLA Ops:
  4.1 15.3 %collective-permute-start.4 = (bf16[8,2,128,128]{3,2,1,0:T(8,128)(2,1)}, bf16[8,2,128,128]{3,2,1,0:T(8,128)(2,1)S(1)}, u32[]{:S(2)}, u32[]{:S(2)}) collective-permute-start(bf16[8,2,128,128]{3,2,1,0:T(8,128)(2,1)} %pad_maximum_fusion.1.same0), channel_id=1, source_target_pairs={{0,16},{8,24},{16,32},{24,40},{32,48},{40,56},{48,64},{56,72},{64,... | collective-permute-start | bytes 1572872 | tf_op jit(solution)/shard_map/ppermute | solution.py:395
  8.8 16.2 %collective-permute-start = (bf16[4,2,8,8192]{3,2,1,0:T(8,128)(2,1)}, bf16[4,2,8,8192]{3,2,1,0:T(8,128)(2,1)S(1)}, u32[]{:S(2)}, u32[]{:S(2)}) collective-permute-start(bf16[4,2,8,8192]{3,2,1,0:T(8,128)(2,1)} %get-tuple-element.110), channel_id=1, source_target_pairs={{103,97},{111,105},{119,113},{127,121}} | collective-permute-start | bytes 3145736 | tf_op jit(solution)/shard_map/ppermute | solution.py:395
  9.5 11.5 %collective-permute-start.6 = (bf16[8,2,128,128]{3,2,1,0:T(8,128)(2,1)}, bf16[8,2,128,128]{3,2,1,0:T(8,128)(2,1)S(1)}, u32[]{:S(2)}, u32[]{:S(2)}) collective-permute-start(bf16[8,2,128,128]{3,2,1,0:T(8,128)(2,1)} %pad_maximum_fusion.1.same0), channel_id=1, source_target_pairs={{0,8},{8,0},{16,24},{24,16},{32,40},{40,32},{48,56},{56,48},{64,72... | collective-permute-start | bytes 1572872 | tf_op jit(solution)/shard_map/ppermute | solution.py:395
  10.6 32.5 %collective-permute-start.1 = (bf16[4,2,8,8192]{3,2,1,0:T(8,128)(2,1)}, bf16[4,2,8,8192]{3,2,1,0:T(8,128)(2,1)}, u32[]{:S(2)}, u32[]{:S(2)}) collective-permute-start(bf16[4,2,8,8192]{3,2,1,0:T(8,128)(2,1)} %get-tuple-element.111), channel_id=1, source_target_pairs={{103,101},{111,109},{119,117},{127,125}} | collective-permute-start | bytes 3145736 | tf_op jit(solution)/shard_map/ppermute | solution.py:395
  12.3 30.9 %collective-permute-start.2 = (bf16[4,2,8,8192]{3,2,1,0:T(8,128)(2,1)}, bf16[4,2,8,8192]{3,2,1,0:T(8,128)(2,1)}, u32[]{:S(2)}, u32[]{:S(2)}) collective-permute-start(bf16[4,2,8,8192]{3,2,1,0:T(8,128)(2,1)} %get-tuple-element.112), channel_id=1, source_target_pairs={{103,38},{111,46},{119,54},{127,62}} | collective-permute-start | bytes 3145736 | tf_op jit(solution)/shard_map/ppermute | solution.py:395
  19.4 23.8 %collective-permute-start.3 = (bf16[4,2,8,8192]{3,2,1,0:T(8,128)(2,1)}, bf16[4,2,8,8192]{3,2,1,0:T(8,128)(2,1)}, u32[]{:S(2)}, u32[]{:S(2)}) collective-permute-start(bf16[4,2,8,8192]{3,2,1,0:T(8,128)(2,1)} %get-tuple-element.113), channel_id=1, source_target_pairs={{103,39},{111,47},{119,55},{127,63}} | collective-permute-start | bytes 3145736 | tf_op jit(solution)/shard_map/ppermute | solution.py:395
  21.0 13.7 %collective-permute-start.5 = (bf16[8,2,128,128]{3,2,1,0:T(8,128)(2,1)S(1)}, bf16[8,2,128,128]{3,2,1,0:T(8,128)(2,1)S(1)}, u32[]{:S(2)}, u32[]{:S(2)}) collective-permute-start(bf16[8,2,128,128]{3,2,1,0:T(8,128)(2,1)S(1)} %collective-permute-done.4.same1), channel_id=1, source_target_pairs={{0,16},{8,24},{16,32},{24,40},{32,48},{40,56},{48,64},{56,72},{64,... | collective-permute-start | bytes 1572872 | tf_op jit(solution)/shard_map/ppermute | solution.py:395
  25.1 18.1 %collective-permute-start.7 = (bf16[8,2,128,128]{3,2,1,0:T(8,128)(2,1)S(1)}, bf16[8,2,128,128]{3,2,1,0:T(8,128)(2,1)S(1)}, u32[]{:S(2)}, u32[]{:S(2)}) collective-permute-start(bf16[8,2,128,128]{3,2,1,0:T(8,128)(2,1)S(1)} %collective-permute-done.4.same1), channel_id=1, source_target_pairs={{0,8},{8,0},{16,24},{24,16},{32,40},{40,32},{48,56},{56,48},{64,72... | collective-permute-start | bytes 1572872 | tf_op jit(solution)/shard_map/ppermute | solution.py:395
  37.1 21.7 %all-to-all-start = ((bf16[8,2,128,128]{3,2,1,0:T(8,128)(2,1)}), bf16[8,2,128,128]{3,2,1,0:T(8,128)(2,1)S(1)}, u32[]{:S(2)}, u32[]{:S(2)}) async-start(bf16[8,2,128,128]{3,2,1,0:T(8,128)(2,1)} %pad_maximum_fusion.1.same0), calls=%async_computation | async-start | bytes 1048576 | tf_op jit(solution)/shard_map/all_to_all | solution.py:432
  44.1 14.8 %collective-permute-start.9 = (bf16[2,8,8192]{2,1,0:T(8,128)(2,1)}, bf16[2,8,8192]{2,1,0:T(8,128)(2,1)S(1)}, u32[]{:S(2)}, u32[]{:S(2)}) collective-permute-start(bf16[2,8,8192]{2,1,0:T(8,128)(2,1)} %get-tuple-element.119), channel_id=1, source_target_pairs={{97,32},{105,40},{113,48},{121,56},{101,36},{109,44},{117,52},{125... | collective-permute-start | bytes 786440 | tf_op jit(solution)/shard_map/ppermute | solution.py:395
  44.8 14.1 %collective-permute-start.10 = (bf16[2,8,8192]{2,1,0:T(8,128)(2,1)}, bf16[2,8,8192]{2,1,0:T(8,128)(2,1)S(1)}, u32[]{:S(2)}, u32[]{:S(2)}) collective-permute-start(bf16[2,8,8192]{2,1,0:T(8,128)(2,1)} %get-tuple-element.120), channel_id=1, source_target_pairs={{97,96},{105,104},{113,112},{121,120},{101,100},{109,108},{117,116... | collective-permute-start | bytes 786440 | tf_op jit(solution)/shard_map/ppermute | solution.py:395
  45.5 13.4 %collective-permute-start.11 = (bf16[2,8,8192]{2,1,0:T(8,128)(2,1)}, bf16[2,8,8192]{2,1,0:T(8,128)(2,1)S(1)}, u32[]{:S(2)}, u32[]{:S(2)}) collective-permute-start(bf16[2,8,8192]{2,1,0:T(8,128)(2,1)} %get-tuple-element.121), channel_id=1, source_target_pairs={{97,33},{105,41},{113,49},{121,57},{101,37},{109,45},{117,53},{125... | collective-permute-start | bytes 786440 | tf_op jit(solution)/shard_map/ppermute | solution.py:395
  59.8 39.9 %all-to-all-start.1 = ((bf16[8,2,8,1024]{3,2,1,0:T(8,128)(2,1)}), bf16[8,2,8,1024]{3,2,1,0:T(8,128)(2,1)S(1)}, u32[]{:S(2)}, u32[]{:S(2)}) async-start(bf16[8,2,8,1024]{3,2,1,0:T(8,128)(2,1)} %shard_map.86), calls=%async_computation.1 | async-start | bytes 524288 | tf_op jit(solution)/shard_map/all_to_all | solution.py:432
  67.2 51.3 %collective-permute-start.14 = (bf16[8,2,128,128]{3,2,1,0:T(8,128)(2,1)S(1)}, bf16[8,2,128,128]{3,2,1,0:T(8,128)(2,1)S(1)}, u32[]{:S(2)}, u32[]{:S(2)}) collective-permute-start(bf16[8,2,128,128]{3,2,1,0:T(8,128)(2,1)S(1)} %all-to-all-done), channel_id=1, source_target_pairs={{0,6},{8,14},{16,22},{24,30},{32,38},{40,46},{48,54},{56,62},{64,7... | collective-permute-start | bytes 1572872 | tf_op jit(solution)/shard_map/ppermute | solution.py:395
  86.4 32.1 %collective-permute-start.13 = (bf16[8,2,128,128]{3,2,1,0:T(8,128)(2,1)S(1)}, bf16[8,2,128,128]{3,2,1,0:T(8,128)(2,1)S(1)}, u32[]{:S(2)}, u32[]{:S(2)}) collective-permute-start(bf16[8,2,128,128]{3,2,1,0:T(8,128)(2,1)S(1)} %all-to-all-done), channel_id=1, source_target_pairs={{0,4},{8,12},{16,20},{24,28},{32,36},{40,44},{48,52},{56,60},{64,6... | collective-permute-start | bytes 1572872 | tf_op jit(solution)/shard_map/ppermute | solution.py:395
  86.4 32.1 %collective-permute-start.12 = (bf16[8,2,128,128]{3,2,1,0:T(8,128)(2,1)S(1)}, bf16[8,2,128,128]{3,2,1,0:T(8,128)(2,1)S(1)}, u32[]{:S(2)}, u32[]{:S(2)}) collective-permute-start(bf16[8,2,128,128]{3,2,1,0:T(8,128)(2,1)S(1)} %all-to-all-done), channel_id=1, source_target_pairs={{0,2},{8,10},{16,18},{24,26},{32,34},{40,42},{48,50},{56,58},{64,6... | collective-permute-start | bytes 1572872 | tf_op jit(solution)/shard_map/ppermute | solution.py:395
  100.6 19.6 %all-to-all-start.2 = ((bf16[16,2,8,1024]{3,2,1,0:T(8,128)(2,1)}), bf16[16,2,8,1024]{3,2,1,0:T(8,128)(2,1)S(1)}, u32[]{:S(2)}, u32[]{:S(2)}) async-start(bf16[16,2,8,1024]{3,2,1,0:T(8,128)(2,1)} %bitcast.7), calls=%async_computation.2 | async-start | bytes 1048576 | tf_op jit(solution)/shard_map/all_to_all | solution.py:432
  139.7 16.8 %all-to-all-start.3 = ((f32[4,24,256]{2,1,0:T(8,128)}), f32[4,24,256]{2,1,0:T(8,128)S(1)}, u32[]{:S(2)}, u32[]{:S(2)}) async-start(f32[4,24,256]{2,1,0:T(8,128)} %broadcast_in_dim.7), calls=%async_computation.3 | async-start | bytes 196608 | tf_op jit(solution)/shard_map/all_to_all | solution.py:432
  177.9 16.0 %all-to-all-start.4 = ((bf16[16,2,8,1024]{3,2,1,0:T(8,128)(2,1)}), bf16[16,2,8,1024]{3,2,1,0:T(8,128)(2,1)S(1)}, u32[]{:S(2)}, u32[]{:S(2)}) async-start(bf16[16,2,8,1024]{3,2,1,0:T(8,128)(2,1)} %get-tuple-element.205), calls=%async_computation.4 | async-start | bytes 1048576 | tf_op jit(solution)/shard_map/all_to_all | solution.py:432
  184.7 17.9 %collective-permute-start.23 = (bf16[8,2,128,128]{3,2,1,0:T(8,128)(2,1)S(1)}, bf16[8,2,128,128]{3,2,1,0:T(8,128)(2,1)}, u32[]{:S(2)}, u32[]{:S(2)}) collective-permute-start(bf16[8,2,128,128]{3,2,1,0:T(8,128)(2,1)S(1)} %copy-done.9), channel_id=1, source_target_pairs={{0,8},{8,0},{16,24},{24,16},{32,40},{40,32},{48,56},{56,48},{64,72... | collective-permute-start | bytes 1572872 | tf_op jit(solution)/shard_map/ppermute | solution.py:395
  187.0 29.7 %collective-permute-start.22 = (bf16[8,2,128,128]{3,2,1,0:T(8,128)(2,1)S(1)}, bf16[8,2,128,128]{3,2,1,0:T(8,128)(2,1)}, u32[]{:S(2)}, u32[]{:S(2)}) collective-permute-start(bf16[8,2,128,128]{3,2,1,0:T(8,128)(2,1)S(1)} %copy-done.8), channel_id=1, source_target_pairs={{0,8},{8,0},{16,24},{24,16},{32,40},{40,32},{48,56},{56,48},{64,72... | collective-permute-start | bytes 1572872 | tf_op jit(solution)/shard_map/ppermute | solution.py:395
  194.7 14.4 %all-to-all-start.5 = ((bf16[8,2,8,1024]{3,2,1,0:T(8,128)(2,1)}), bf16[8,2,8,1024]{3,2,1,0:T(8,128)(2,1)S(1)}, u32[]{:S(2)}, u32[]{:S(2)}) async-start(bf16[8,2,8,1024]{3,2,1,0:T(8,128)(2,1)} %concatenate.7), calls=%async_computation.5 | async-start | bytes 524288 | tf_op jit(solution)/shard_map/all_to_all | solution.py:432
  204.8 15.3 %collective-permute-start.24 = (bf16[8,2,128,128]{3,2,1,0:T(8,128)(2,1)}, bf16[8,2,128,128]{3,2,1,0:T(8,128)(2,1)S(1)}, u32[]{:S(2)}, u32[]{:S(2)}) collective-permute-start(bf16[8,2,128,128]{3,2,1,0:T(8,128)(2,1)} %add_convert_fusion.2), channel_id=1, source_target_pairs={{16,0},{24,8},{32,16},{40,24},{48,32},{56,40},{64,48},{72,56},{80,... | collective-permute-start | bytes 1572872 | tf_op jit(solution)/shard_map/ppermute | solution.py:395
  211.5 13.7 %collective-permute-start.28 = (bf16[8,2,128,128]{3,2,1,0:T(8,128)(2,1)S(1)}, bf16[8,2,128,128]{3,2,1,0:T(8,128)(2,1)S(1)}, u32[]{:S(2)}, u32[]{:S(2)}) collective-permute-start(bf16[8,2,128,128]{3,2,1,0:T(8,128)(2,1)S(1)} %get-tuple-element.231), channel_id=1, source_target_pairs={{0,2},{8,10},{16,18},{24,26},{32,34},{40,42},{48,50},{56,58},{64,6... | collective-permute-start | bytes 1572872 | tf_op jit(solution)/shard_map/ppermute | solution.py:395
  212.9 24.2 %collective-permute-start.27 = (bf16[8,2,128,128]{3,2,1,0:T(8,128)(2,1)S(1)}, bf16[8,2,128,128]{3,2,1,0:T(8,128)(2,1)S(1)}, u32[]{:S(2)}, u32[]{:S(2)}) collective-permute-start(bf16[8,2,128,128]{3,2,1,0:T(8,128)(2,1)S(1)} %get-tuple-element.232), channel_id=1, source_target_pairs={{0,4},{8,12},{16,20},{24,28},{32,36},{40,44},{48,52},{56,60},{64,6... | collective-permute-start | bytes 1572872 | tf_op jit(solution)/shard_map/ppermute | solution.py:395
  214.2 30.8 %collective-permute-start.26 = (bf16[8,2,128,128]{3,2,1,0:T(8,128)(2,1)S(1)}, bf16[8,2,128,128]{3,2,1,0:T(8,128)(2,1)S(1)}, u32[]{:S(2)}, u32[]{:S(2)}) collective-permute-start(bf16[8,2,128,128]{3,2,1,0:T(8,128)(2,1)S(1)} %get-tuple-element.230), channel_id=1, source_target_pairs={{0,6},{8,14},{16,22},{24,30},{32,38},{40,46},{48,54},{56,62},{64,7... | collective-permute-start | bytes 1572872 | tf_op jit(solution)/shard_map/ppermute | solution.py:395
  216.7 50.9 %collective-permute-start.18 = (bf16[4,2,8,8192]{3,2,1,0:T(8,128)(2,1)}, bf16[4,2,8,8192]{3,2,1,0:T(8,128)(2,1)}, u32[]{:S(2)}, u32[]{:S(2)}) collective-permute-start(bf16[4,2,8,8192]{3,2,1,0:T(8,128)(2,1)} %maximum_select_fusion), channel_id=1, source_target_pairs={{97,103},{105,111},{113,119},{121,127}} | collective-permute-start | bytes 3145736 | tf_op jit(solution)/shard_map/ppermute | solution.py:395
  220.1 47.5 %collective-permute-start.19 = (bf16[4,2,8,8192]{3,2,1,0:T(8,128)(2,1)}, bf16[4,2,8,8192]{3,2,1,0:T(8,128)(2,1)}, u32[]{:S(2)}, u32[]{:S(2)}) collective-permute-start(bf16[4,2,8,8192]{3,2,1,0:T(8,128)(2,1)} %maximum_select_fusion), channel_id=1, source_target_pairs={{101,103},{109,111},{117,119},{125,127}} | collective-permute-start | bytes 3145736 | tf_op jit(solution)/shard_map/ppermute | solution.py:395
  225.2 42.4 %collective-permute-start.20 = (bf16[4,2,8,8192]{3,2,1,0:T(8,128)(2,1)}, bf16[4,2,8,8192]{3,2,1,0:T(8,128)(2,1)}, u32[]{:S(2)}, u32[]{:S(2)}) collective-permute-start(bf16[4,2,8,8192]{3,2,1,0:T(8,128)(2,1)} %maximum_select_fusion), channel_id=1, source_target_pairs={{38,103},{46,111},{54,119},{62,127}} | collective-permute-start | bytes 3145736 | tf_op jit(solution)/shard_map/ppermute | solution.py:395
  237.1 30.5 %collective-permute-start.21 = (bf16[4,2,8,8192]{3,2,1,0:T(8,128)(2,1)}, bf16[4,2,8,8192]{3,2,1,0:T(8,128)(2,1)}, u32[]{:S(2)}, u32[]{:S(2)}) collective-permute-start(bf16[4,2,8,8192]{3,2,1,0:T(8,128)(2,1)} %maximum_select_fusion), channel_id=1, source_target_pairs={{39,103},{47,111},{55,119},{63,127}} | collective-permute-start | bytes 3145736 | tf_op jit(solution)/shard_map/ppermute | solution.py:395
  245.0 15.3 %collective-permute-start.25 = (bf16[8,2,128,128]{3,2,1,0:T(8,128)(2,1)}, bf16[8,2,128,128]{3,2,1,0:T(8,128)(2,1)}, u32[]{:S(2)}, u32[]{:S(2)}) collective-permute-start(bf16[8,2,128,128]{3,2,1,0:T(8,128)(2,1)} %add_convert_fusion.1), channel_id=1, source_target_pairs={{16,0},{24,8},{32,16},{40,24},{48,32},{56,40},{64,48},{72,56},{80,... | collective-permute-start | bytes 1572872 | tf_op jit(solution)/shard_map/ppermute | solution.py:395
  247.4 16.7 %all-to-all-start.6 = ((bf16[8,2,128,128]{3,2,1,0:T(8,128)(2,1)}), bf16[8,2,128,128]{3,2,1,0:T(8,128)(2,1)S(1)}, u32[]{:S(2)}, u32[]{:S(2)}) async-start(bf16[8,2,128,128]{3,2,1,0:T(8,128)(2,1)} %fusion.2), calls=%async_computation.6 | async-start | bytes 1048576 | tf_op jit(solution)/shard_map/all_to_all | solution.py:432
  (20 other events, 252.2 us)
where the time goes:
time: 272 us; the launch traced here: 268 us
  starting transfers between devices  104 us (38%)
  Pallas kernels  89.6 us (33%)
  waiting for transfers between devices  51.9 us (19%)
  other arithmetic  11.3 us (4%)
  local copies, waits for them, and re-layouts  10.3 us (4%)
    ppermute x29, starting transfers between devices, permuted(): lax.ppermute(block, MESH_AXES, [(index[i], index[j]) for i, j in pairs])  58.9 us
    pallas_call x4, Pallas kernels, context_attention(): pl.pallas_call(context_kernel, grid_spec=pltpu.PrefetchScalarGridSpec(num...  50.8 us
    all_to_all x7, starting transfers between devices, exchanged(): return lax.all_to_all(blocks, axes, split_axis=0, concat_axis=0, tiled=True)  44.7 us
    ppermute x29, waiting for transfers between devices, permuted(): lax.ppermute(block, MESH_AXES, [(index[i], index[j]) for i, j in pairs])  38.5 us
    pallas_call x1, Pallas kernels, question_attention(): pl.pallas_call(question_kernel, grid_spec=pltpu.PrefetchScalarGridSpec(nu...  20.7 us
    pallas_call x1, Pallas kernels, question_statistics(): pl.pallas_call(statistics_kernel, grid_spec=pltpu.PrefetchScalarGridSpec(...  17.4 us
    all_to_all x7, waiting for transfers between devices, exchanged(): return lax.all_to_all(blocks, axes, split_axis=0, concat_axis=0, tiled=True)  13.5 us
    unnamed x36, local copies, waits for them, and re-layouts  6.4 us
  transfers between devices with their start and end apart: 36, of which 10 were waited for; matrix products, arithmetic and copies ran while one was open for 5% of the time, Pallas kernels for 19%

commit v1 on v0

--- a/solution.py
+++ b/solution.py
@@ -60,8 +60,8 @@
 def context_kernel(
     place_ref, span_ref, q_ref, g_ref, same0, same1, same2, swapped0, swapped1, swapped2, *rest,
 ):
-    rest = rest[-14:]
-    out_ref, dq_ref, d0, d1, d2, d3, d4, bias, k_win, v_win, k_t, v_t, dk_acc, dv_acc = rest
+    rest = rest[-16:]
+    out_ref, dq_ref, d0, d1, d2, d3, d4, bias, k_win, v_win, k_t, v_t, p_all, ds_all, q_all, g_all = rest
     window = (BACK + 1) * ROWS
     group, pair = pl.program_id(0), pl.program_id(1)
     place = place_ref[0]
@@ -91,8 +91,6 @@
         fill(0, same2)
         fill(2, same1)
         fill(4, same0)
-        dk_acc[...] = jnp.zeros_like(dk_acc)
-        dv_acc[...] = jnp.zeros_like(dv_acc)
 
     @pl.when((pair == 0) & (place % 2 == 0))
     def _():
@@ -104,33 +102,38 @@
         fill(1, swapped1)
         fill(3, swapped0)
 
-    q = stacked(q_ref[...])
-    g = stacked(g_ref[...])
     hide = jnp.concatenate([bias[...], bias[...]], axis=1)
-    s = dot_nt(k_win[...], q) * SCALE2 + hide
-    top = jnp.maximum(jnp.max(s, axis=0, keepdims=True), FLOOR)
-    w = jnp.exp2(s - top)
-    total = jnp.sum(w, axis=0, keepdims=True)
-    p = w * jnp.where(total > 0.0, 1.0 / total, 0.0)
-    dp = dot_nt(v_win[...], g)
-    dd = jnp.sum(p * dp, axis=0, keepdims=True)
-    ds = (p * (dp - dd)).astype(BF16)
-    pb = p.astype(BF16)
-    out_ref[...] = unstacked(dot_nn(v_t[...], pb))
-    dq_ref[...] = unstacked(dot_nn(k_t[...], ds) * SCALE)
-    dv_acc[...] += dot_nn(pb, g)
-    dk_acc[...] += dot_nn(ds, q)
-
-    @pl.when(pair == GROUP // 2 - 1)
-    def _():
-        for i, ref in enumerate((d4, d3, d2, d1, d0)):
-            ref[0, 0] = (dk_acc[i * ROWS : (i + 1) * ROWS] * SCALE).astype(BF16)
-            ref[0, 1] = dv_acc[i * ROWS : (i + 1) * ROWS].astype(BF16)
+    kw, vw = k_win[...], v_win[...]
+    for n in range(GROUP // 2):
+        cols = slice(2 * n * HEAD_WIDTH, 2 * (n + 1) * HEAD_WIDTH)
+        lanes = slice(2 * n * ROWS, 2 * (n + 1) * ROWS)
+        q = stacked(q_ref[:, cols])
+        g = stacked(g_ref[:, cols])
+        s = dot_nt(kw, q) * SCALE2 + hide
+        dp = dot_nt(vw, g)
+        top = jnp.maximum(jnp.max(s, axis=0, keepdims=True), FLOOR)
+        w = jnp.exp2(s - top)
+        total = jnp.sum(w, axis=0, keepdims=True)
+        p = w * jnp.where(total > 0.0, 1.0 / total, 0.0)
+        dd = jnp.sum(p * dp, axis=0, keepdims=True)
+        ds = (p * (dp - dd)).astype(BF16)
+        pb = p.astype(BF16)
+        out_ref[:, cols] = unstacked(dot_nn(v_t[...], pb))
+        dq_ref[:, cols] = unstacked(dot_nn(k_t[...], ds) * SCALE)
+        p_all[:, lanes] = pb
+        ds_all[:, lanes] = ds
+        q_all[lanes] = q
+        g_all[lanes] = g
+    dk = dot_nn(ds_all[...], q_all[...]) * SCALE
+    dv = dot_nn(p_all[...], g_all[...])
+    for i, ref in enumerate((d4, d3, d2, d1, d0)):
+        ref[0, 0] = dk[i * ROWS : (i + 1) * ROWS].astype(BF16)
+        ref[0, 1] = dv[i * ROWS : (i + 1) * ROWS].astype(BF16)
 
 
 def context_attention(first, count, place, span_lengths, q, g, blocks, before=()):
     window = (BACK + 1) * ROWS
-    wide = pl.BlockSpec((ROWS, 2 * HEAD_WIDTH), lambda a, b, *_: (0, (a + first) * (GROUP // 2) + b))
+    wide = pl.BlockSpec((ROWS, GROUP * HEAD_WIDTH), lambda a, b, *_: (0, a + first))
     block = pl.BlockSpec((1, 2, ROWS, HEAD_WIDTH), lambda a, b, *_: (a + first, 0, 0, 0))
     whole = jax.ShapeDtypeStruct(q.shape, BF16)
     part = jax.ShapeDtypeStruct((KEY_VALUE_HEADS, 2, ROWS, HEAD_WIDTH), BF16)
@@ -138,7 +141,7 @@
         context_kernel,
         grid_spec=pltpu.PrefetchScalarGridSpec(
             num_scalar_prefetch=2,
-            grid=(count, GROUP // 2),
+            grid=(count, 1),
             in_specs=[wide, wide] + [block] * 6 + [pl.BlockSpec(memory_space=pl.ANY)] * len(before),
             out_specs=[wide, wide] + [block] * 5,
             scratch_shapes=[
@@ -147,8 +150,10 @@
                 pltpu.VMEM((window, HEAD_WIDTH), BF16),
                 pltpu.VMEM((HEAD_WIDTH, window), BF16),
                 pltpu.VMEM((HEAD_WIDTH, window), BF16),
-                pltpu.VMEM((window, HEAD_WIDTH), F32),
-                pltpu.VMEM((window, HEAD_WIDTH), F32),
+                pltpu.VMEM((window, GROUP * ROWS), BF16),
+                pltpu.VMEM((window, GROUP * ROWS), BF16),
+                pltpu.VMEM((GROUP * ROWS, HEAD_WIDTH), BF16),
+                pltpu.VMEM((GROUP * ROWS, HEAD_WIDTH), BF16),
             ],
         ),
         out_shape=[whole, whole] + [part] * 5,
@@ -459,7 +464,10 @@
     kv = jnp.stack([headed(k), headed(v)], axis=1)
     kv_ring = exchanged(kv, ("z", "c"))
     pieces = question_pieces(place_arg, q, g)
-    pieces = [permuted(pieces[j], hub_pairs(j)) for j in range(4)]
+    dealt = {}
+    for j in range(4):
+        dealt[j] = permuted(pieces[j], hub_pairs(j))
+    pieces = [dealt[j] for j in range(4)]
     same1 = shifted(kv, 2)
     same2 = shifted(same1, 2)
     blocks = (kv, same1, same2, swapped(kv), swapped(same1), swapped(same2))

time: 272 us -> 266 us (0.978)
  Pallas kernels: 89.6 us -> 80.9 us
    pallas_call x4, Pallas kernels: 50.8 us -> 42.1 us  [context_attention(): pl.pallas_call(context_kernel, grid_spec=pltpu.PrefetchScalarGridSpec(num...]
    all_to_all x7, starting transfers between devices: 44.7 us -> 48.7 us  [exchanged(): return lax.all_to_all(blocks, axes, split_axis=0, concat_axis=0, tiled=True)]
  transfers between devices with their start and end apart: 36 -> 36, of which waited for: 10 -> 11; matrix products, arithmetic and copies ran while one was open for 5% -> 5% of each run, Pallas kernels for 19% -> 16%
where the time goes in v1:
time: 266 us; the launch traced here: 262 us
  starting transfers between devices  106 us (40%)
  Pallas kernels  80.9 us (30%)
  waiting for transfers between devices  52 us (20%)
  other arithmetic  11.3 us (4%)
  local copies, waits for them, and re-layouts  10.3 us (4%)
    ppermute x29, starting transfers between devices, permuted(): lax.ppermute(block, MESH_AXES, [(index[i], index[j]) for i, j in pairs])  56.9 us
    all_to_all x7, starting transfers between devices, exchanged(): return lax.all_to_all(blocks, axes, split_axis=0, concat_axis=0, tiled=True)  48.7 us
    pallas_call x4, Pallas kernels, context_attention(): pl.pallas_call(context_kernel, grid_spec=pltpu.PrefetchScalarGridSpec(num...  42.1 us
    ppermute x29, waiting for transfers between devices, permuted(): lax.ppermute(block, MESH_AXES, [(index[i], index[j]) for i, j in pairs])  38.2 us
    pallas_call x1, Pallas kernels, question_attention(): pl.pallas_call(question_kernel, grid_spec=pltpu.PrefetchScalarGridSpec(nu...  20.7 us
    pallas_call x1, Pallas kernels, question_statistics(): pl.pallas_call(statistics_kernel, grid_spec=pltpu.PrefetchScalarGridSpec(...  17.4 us
    all_to_all x7, waiting for transfers between devices, exchanged(): return lax.all_to_all(blocks, axes, split_axis=0, concat_axis=0, tiled=True)  13.8 us
    unnamed x36, local copies, waits for them, and re-layouts  6.4 us
  transfers between devices with their start and end apart: 36, of which 11 were waited for; matrix products, arithmetic and copies ran while one was open for 5% of the time, Pallas kernels for 16%

profile of v1, /device:TPU:1, one launch (start us, length us, event | category | flops | bytes accessed | tf_op | source)
XLA Modules:
  0.0 261.5 jit_solution(934881856510884109)
XLA Ops:
  4.1 4.4 %collective-permute-start.4 = (bf16[8,2,128,128]{3,2,1,0:T(8,128)(2,1)}, bf16[8,2,128,128]{3,2,1,0:T(8,128)(2,1)S(1)}, u32[]{:S(2)}, u32[]{:S(2)}) collective-permute-start(bf16[8,2,128,128]{3,2,1,0:T(8,128)(2,1)} %pad_maximum_fusion.1.same0), channel_id=1, source_target_pairs={{0,16},{8,24},{16,32},{24,40},{32,48},{40,56},{48,64},{56,72},{64,... | collective-permute-start | bytes 1572872 | tf_op jit(solution)/shard_map/ppermute | solution.py:400
  10.6 1.7 collective-permute-start.1
  13.9 5.5 %collective-permute-done.4.same1 = bf16[8,2,128,128]{3,2,1,0:T(8,128)(2,1)S(1)} collective-permute-done((bf16[8,2,128,128]{3,2,1,0:T(8,128)(2,1)}, bf16[8,2,128,128]{3,2,1,0:T(8,128)(2,1)S(1)}, u32[]{:S(2)}, u32[]{:S(2)}) %collective-permute-start.4) | collective-permute-done | bytes 524320 | tf_op jit(solution)/shard_map/ppermute | solution.py:400
  21.0 4.0 %collective-permute-start.5 = (bf16[8,2,128,128]{3,2,1,0:T(8,128)(2,1)S(1)}, bf16[8,2,128,128]{3,2,1,0:T(8,128)(2,1)S(1)}, u32[]{:S(2)}, u32[]{:S(2)}) collective-permute-start(bf16[8,2,128,128]{3,2,1,0:T(8,128)(2,1)S(1)} %collective-permute-done.4.same1), channel_id=1, source_target_pairs={{0,16},{8,24},{16,32},{24,40},{32,48},{40,56},{48,64},{56,72},{64,... | collective-permute-start | bytes 1572872 | tf_op jit(solution)/shard_map/ppermute | solution.py:400
  25.1 1.9 collective-permute-start.7
  27.0 7.8 %collective-permute-done.5.same2 = bf16[8,2,128,128]{3,2,1,0:T(8,128)(2,1)S(1)} collective-permute-done((bf16[8,2,128,128]{3,2,1,0:T(8,128)(2,1)S(1)}, bf16[8,2,128,128]{3,2,1,0:T(8,128)(2,1)S(1)}, u32[]{:S(2)}, u32[]{:S(2)}) %collective-permute-start.5) | collective-permute-done | bytes 524320 | tf_op jit(solution)/shard_map/ppermute | solution.py:400
  34.7 2.4 collective-permute-start.8
  37.1 6.0 %all-to-all-start = ((bf16[8,2,128,128]{3,2,1,0:T(8,128)(2,1)}), bf16[8,2,128,128]{3,2,1,0:T(8,128)(2,1)S(1)}, u32[]{:S(2)}, u32[]{:S(2)}) async-start(bf16[8,2,128,128]{3,2,1,0:T(8,128)(2,1)} %pad_maximum_fusion.1.same0), calls=%async_computation | async-start | bytes 1048576 | tf_op jit(solution)/shard_map/all_to_all | solution.py:437
  46.2 10.5 %context_rows.4 = (bf16[128,8192]{1,0:T(8,128)(2,1)}, bf16[128,8192]{1,0:T(8,128)(2,1)}, bf16[8,2,128,128]{3,2,1,0:T(8,128)(2,1)}, bf16[8,2,128,128]{3,2,1,0:T(8...) custom-call(s32[1]{0:T(128)} %bitcast.place_ref, ...), custom_call_target="tpu_custom_call" | custom-call | tf_op jit(solution)/shard_map/context_rows/pallas_call | solution.py:140
  57.7 9.5 %all-to-all-start.1 = ((bf16[8,2,8,1024]{3,2,1,0:T(8,128)(2,1)}), bf16[8,2,8,1024]{3,2,1,0:T(8,128)(2,1)S(1)}, u32[]{:S(2)}, u32[]{:S(2)}) async-start(bf16[8,2,8,1024]{3,2,1,0:T(8,128)(2,1)} %shard_map.86), calls=%async_computation.1 | async-start | bytes 524288 | tf_op jit(solution)/shard_map/all_to_all | solution.py:437
  67.2 17.1 %collective-permute-start.14 = (bf16[8,2,128,128]{3,2,1,0:T(8,128)(2,1)S(1)}, bf16[8,2,128,128]{3,2,1,0:T(8,128)(2,1)S(1)}, u32[]{:S(2)}, u32[]{:S(2)}) collective-permute-start(bf16[8,2,128,128]{3,2,1,0:T(8,128)(2,1)S(1)} %all-to-all-done), channel_id=1, source_target_pairs={{0,6},{8,14},{16,22},{24,30},{32,38},{40,46},{48,54},{56,62},{64,7... | collective-permute-start | bytes 1572872 | tf_op jit(solution)/shard_map/ppermute | solution.py:400
  84.9 10.5 %context_rows.5 = (bf16[128,8192]{1,0:T(8,128)(2,1)}, bf16[128,8192]{1,0:T(8,128)(2,1)}, bf16[8,2,128,128]{3,2,1,0:T(8,128)(2,1)}, bf16[8,2,128,128]{3,2,1,0:T(8...) custom-call(s32[1]{0:T(128)} %bitcast.place_ref, ...), custom_call_target="tpu_custom_call", output_to_operand_aliasing={{0}: (10, {}), {1}: (11, {}), {2}: (12, {}), {3}: (13, {}),... | custom-call | tf_op jit(solution)/shard_map/context_rows/pallas_call | solution.py:140
  96.3 7.4 %all-to-all-start.2 = ((bf16[16,2,8,1024]{3,2,1,0:T(8,128)(2,1)}), bf16[16,2,8,1024]{3,2,1,0:T(8,128)(2,1)S(1)}, u32[]{:S(2)}, u32[]{:S(2)}) async-start(bf16[16,2,8,1024]{3,2,1,0:T(8,128)(2,1)} %bitcast.7), calls=%async_computation.2 | async-start | bytes 1048576 | tf_op jit(solution)/shard_map/all_to_all | solution.py:437
  103.6 10.5 %context_rows.6 = (bf16[128,8192]{1,0:T(8,128)(2,1)}, bf16[128,8192]{1,0:T(8,128)(2,1)}, bf16[8,2,128,128]{3,2,1,0:T(8,128)(2,1)}, bf16[8,2,128,128]{3,2,1,0:T(8...) custom-call(s32[1]{0:T(128)} %bitcast.place_ref, ...), custom_call_target="tpu_custom_call", output_to_operand_aliasing={{0}: (10, {}), {1}: (11, {}), {2}: (12, {}), {3}: (13, {}),... | custom-call | tf_op jit(solution)/shard_map/context_rows/pallas_call | solution.py:140
  116.9 17.4 %question_statistics.1 = f32[24,256]{1,0:T(8,128)} custom-call(s32[1]{0:T(128)} %bitcast.place_ref, bf16[16,2,8,1024]{3,2,1,0:T(8,128)(2,1)} %copy-done.10, bf16[4,8,2,128,128]{4,3,2,1,0:T(8,128)(2,1)} %pad_maximum_fusion.kv_ref), custom_call_target="tpu_custom_call" | custom-call | tf_op jit(solution)/shard_map/question_statistics/pallas_call | solution.py:255
  135.6 3.9 %all-to-all-start.3 = ((f32[4,24,256]{2,1,0:T(8,128)}), f32[4,24,256]{2,1,0:T(8,128)S(1)}, u32[]{:S(2)}, u32[]{:S(2)}) async-start(f32[4,24,256]{2,1,0:T(8,128)} %broadcast_in_dim.7), calls=%async_computation.3 | async-start | bytes 196608 | tf_op jit(solution)/shard_map/all_to_all | solution.py:437
  139.5 10.5 %context_rows.7 = (bf16[128,8192]{1,0:T(8,128)(2,1)}, bf16[128,8192]{1,0:T(8,128)(2,1)}, bf16[8,2,128,128]{3,2,1,0:T(8,128)(2,1)}, bf16[8,2,128,128]{3,2,1,0:T(8...) custom-call(s32[1]{0:T(128)} %bitcast.place_ref, ...), custom_call_target="tpu_custom_call", output_to_operand_aliasing={{0}: (10, {}), {1}: (11, {}), {2}: (12, {}), {3}: (13, {}),... | custom-call | tf_op jit(solution)/shard_map/context_rows/pallas_call | solution.py:140
  150.7 20.7 %question_rows.1 = (bf16[16,2,8,1024]{3,2,1,0:T(8,128)(2,1)}, bf16[4,8,2,128,128]{4,3,2,1,0:T(8,128)(2,1)}) custom-call(s32[1]{0:T(128)} %bitcast.place_ref, bf16[16,2,8,1024]{3,2,1,0:T(8,128)(2,1)} %copy-done.10, bf16[4,8,2,128,128]{4,3,2,1,0:T(8,128)(2,1)} %pad_maximum_fusion.kv_ref, f32[16,256]{1,0:T(8,128)} %pad_maximum_fusion.2.stats_ref), custom_call_target="tpu_custom_call" | custom-call | tf_op jit(solution)/shard_map/question_rows/pallas_call | solution.py:277
  171.4 6.8 %all-to-all-start.4 = ((bf16[16,2,8,1024]{3,2,1,0:T(8,128)(2,1)}), bf16[16,2,8,1024]{3,2,1,0:T(8,128)(2,1)S(1)}, u32[]{:S(2)}, u32[]{:S(2)}) async-start(bf16[16,2,8,1024]{3,2,1,0:T(8,128)(2,1)} %get-tuple-element.205), calls=%async_computation.4 | async-start | bytes 1048576 | tf_op jit(solution)/shard_map/all_to_all | solution.py:437
  178.2 2.2 collective-permute-start.23
  180.6 6.8 %all-to-all-done.4 = bf16[16,2,8,1024]{3,2,1,0:T(8,128)(2,1)S(1)} async-done(((bf16[16,2,8,1024]{3,2,1,0:T(8,128)(2,1)}), bf16[16,2,8,1024]{3,2,1,0:T(8,128)(2,1)S(1)}, u32[]{:S(2)}, u32[]{:S(2)}) %all-to-all-start.4) | async-done | bytes 524320 | tf_op jit(solution)/shard_map/all_to_all | solution.py:437
  188.2 7.9 %all-to-all-start.5 = ((bf16[8,2,8,1024]{3,2,1,0:T(8,128)(2,1)}), bf16[8,2,8,1024]{3,2,1,0:T(8,128)(2,1)S(1)}, u32[]{:S(2)}, u32[]{:S(2)}) async-start(bf16[8,2,8,1024]{3,2,1,0:T(8,128)(2,1)} %concatenate.7), calls=%async_computation.5 | async-start | bytes 524288 | tf_op jit(solution)/shard_map/all_to_all | solution.py:437
  196.0 2.2 add_convert_fusion.2
  199.5 3.0 %all-to-all-done.5 = bf16[8,2,8,1024]{3,2,1,0:T(8,128)(2,1)S(1)} async-done(((bf16[8,2,8,1024]{3,2,1,0:T(8,128)(2,1)}), bf16[8,2,8,1024]{3,2,1,0:T(8,128)(2,1)S(1)}, u32[]{:S(2)}, u32[]{:S(2)}) %all-to-all-start.5) | async-done | bytes 262176 | tf_op jit(solution)/shard_map/all_to_all | solution.py:437
  210.3 1.7 collective-permute-start.18
  215.2 2.2 add_convert_fusion.1
  220.2 10.4 %collective-permute-done.27 = bf16[8,2,128,128]{3,2,1,0:T(8,128)(2,1)S(1)} collective-permute-done((bf16[8,2,128,128]{3,2,1,0:T(8,128)(2,1)S(1)}, bf16[8,2,128,128]{3,2,1,0:T(8,128)(2,1)S(1)}, u32[]{:S(2)}, u32[]{:S(2)}) %collective-permute-start.27) | collective-permute-done | bytes 524320 | tf_op jit(solution)/shard_map/ppermute | solution.py:400
  230.6 1.7 collective-permute-start.21
  232.3 6.1 %collective-permute-done.26 = bf16[8,2,128,128]{3,2,1,0:T(8,128)(2,1)S(1)} collective-permute-done((bf16[8,2,128,128]{3,2,1,0:T(8,128)(2,1)S(1)}, bf16[8,2,128,128]{3,2,1,0:T(8,128)(2,1)S(1)}, u32[]{:S(2)}, u32[]{:S(2)}) %collective-permute-start.26) | collective-permute-done | bytes 524320 | tf_op jit(solution)/shard_map/ppermute | solution.py:400
  240.8 7.3 %all-to-all-start.6 = ((bf16[8,2,128,128]{3,2,1,0:T(8,128)(2,1)}), bf16[8,2,128,128]{3,2,1,0:T(8,128)(2,1)S(1)}, u32[]{:S(2)}, u32[]{:S(2)}) async-start(bf16[8,2,128,128]{3,2,1,0:T(8,128)(2,1)} %fusion.2), calls=%async_computation.6 | async-start | bytes 1048576 | tf_op jit(solution)/shard_map/all_to_all | solution.py:437
  248.1 5.6 %collective-permute-done.25 = bf16[8,2,128,128]{3,2,1,0:T(8,128)(2,1)} collective-permute-done((bf16[8,2,128,128]{3,2,1,0:T(8,128)(2,1)}, bf16[8,2,128,128]{3,2,1,0:T(8,128)(2,1)}, u32[]{:S(2)}, u32[]{:S(2)}) %collective-permute-start.25) | collective-permute-done | bytes 524320 | tf_op jit(solution)/shard_map/ppermute | solution.py:400
  253.7 3.8 %all-to-all-done.6 = bf16[8,2,128,128]{3,2,1,0:T(8,128)(2,1)S(1)} async-done(((bf16[8,2,128,128]{3,2,1,0:T(8,128)(2,1)}), bf16[8,2,128,128]{3,2,1,0:T(8,128)(2,1)S(1)}, u32[]{:S(2)}, u32[]{:S(2)}) %all-to-all-start.6) | async-done | bytes 524320 | tf_op jit(solution)/shard_map/all_to_all | solution.py:437
  (109 shorter events, 41.1 us)
Async XLA Ops:
  4.1 15.3 %collective-permute-start.4 = (bf16[8,2,128,128]{3,2,1,0:T(8,128)(2,1)}, bf16[8,2,128,128]{3,2,1,0:T(8,128)(2,1)S(1)}, u32[]{:S(2)}, u32[]{:S(2)}) collective-permute-start(bf16[8,2,128,128]{3,2,1,0:T(8,128)(2,1)} %pad_maximum_fusion.1.same0), channel_id=1, source_target_pairs={{0,16},{8,24},{16,32},{24,40},{32,48},{40,56},{48,64},{56,72},{64,... | collective-permute-start | bytes 1572872 | tf_op jit(solution)/shard_map/ppermute | solution.py:400
  8.8 16.2 %collective-permute-start = (bf16[4,2,8,8192]{3,2,1,0:T(8,128)(2,1)}, bf16[4,2,8,8192]{3,2,1,0:T(8,128)(2,1)S(1)}, u32[]{:S(2)}, u32[]{:S(2)}) collective-permute-start(bf16[4,2,8,8192]{3,2,1,0:T(8,128)(2,1)} %get-tuple-element.110), channel_id=1, source_target_pairs={{103,97},{111,105},{119,113},{127,121}} | collective-permute-start | bytes 3145736 | tf_op jit(solution)/shard_map/ppermute | solution.py:400
  9.5 11.5 %collective-permute-start.6 = (bf16[8,2,128,128]{3,2,1,0:T(8,128)(2,1)}, bf16[8,2,128,128]{3,2,1,0:T(8,128)(2,1)S(1)}, u32[]{:S(2)}, u32[]{:S(2)}) collective-permute-start(bf16[8,2,128,128]{3,2,1,0:T(8,128)(2,1)} %pad_maximum_fusion.1.same0), channel_id=1, source_target_pairs={{0,8},{8,0},{16,24},{24,16},{32,40},{40,32},{48,56},{56,48},{64,72... | collective-permute-start | bytes 1572872 | tf_op jit(solution)/shard_map/ppermute | solution.py:400
  10.6 32.5 %collective-permute-start.1 = (bf16[4,2,8,8192]{3,2,1,0:T(8,128)(2,1)}, bf16[4,2,8,8192]{3,2,1,0:T(8,128)(2,1)}, u32[]{:S(2)}, u32[]{:S(2)}) collective-permute-start(bf16[4,2,8,8192]{3,2,1,0:T(8,128)(2,1)} %get-tuple-element.111), channel_id=1, source_target_pairs={{103,101},{111,109},{119,117},{127,125}} | collective-permute-start | bytes 3145736 | tf_op jit(solution)/shard_map/ppermute | solution.py:400
  12.3 30.9 %collective-permute-start.2 = (bf16[4,2,8,8192]{3,2,1,0:T(8,128)(2,1)}, bf16[4,2,8,8192]{3,2,1,0:T(8,128)(2,1)}, u32[]{:S(2)}, u32[]{:S(2)}) collective-permute-start(bf16[4,2,8,8192]{3,2,1,0:T(8,128)(2,1)} %get-tuple-element.112), channel_id=1, source_target_pairs={{103,38},{111,46},{119,54},{127,62}} | collective-permute-start | bytes 3145736 | tf_op jit(solution)/shard_map/ppermute | solution.py:400
  19.4 23.8 %collective-permute-start.3 = (bf16[4,2,8,8192]{3,2,1,0:T(8,128)(2,1)}, bf16[4,2,8,8192]{3,2,1,0:T(8,128)(2,1)}, u32[]{:S(2)}, u32[]{:S(2)}) collective-permute-start(bf16[4,2,8,8192]{3,2,1,0:T(8,128)(2,1)} %get-tuple-element.113), channel_id=1, source_target_pairs={{103,39},{111,47},{119,55},{127,63}} | collective-permute-start | bytes 3145736 | tf_op jit(solution)/shard_map/ppermute | solution.py:400
  21.0 13.7 %collective-permute-start.5 = (bf16[8,2,128,128]{3,2,1,0:T(8,128)(2,1)S(1)}, bf16[8,2,128,128]{3,2,1,0:T(8,128)(2,1)S(1)}, u32[]{:S(2)}, u32[]{:S(2)}) collective-permute-start(bf16[8,2,128,128]{3,2,1,0:T(8,128)(2,1)S(1)} %collective-permute-done.4.same1), channel_id=1, source_target_pairs={{0,16},{8,24},{16,32},{24,40},{32,48},{40,56},{48,64},{56,72},{64,... | collective-permute-start | bytes 1572872 | tf_op jit(solution)/shard_map/ppermute | solution.py:400
  25.1 18.1 %collective-permute-start.7 = (bf16[8,2,128,128]{3,2,1,0:T(8,128)(2,1)S(1)}, bf16[8,2,128,128]{3,2,1,0:T(8,128)(2,1)S(1)}, u32[]{:S(2)}, u32[]{:S(2)}) collective-permute-start(bf16[8,2,128,128]{3,2,1,0:T(8,128)(2,1)S(1)} %collective-permute-done.4.same1), channel_id=1, source_target_pairs={{0,8},{8,0},{16,24},{24,16},{32,40},{40,32},{48,56},{56,48},{64,72... | collective-permute-start | bytes 1572872 | tf_op jit(solution)/shard_map/ppermute | solution.py:400
  37.1 19.6 %all-to-all-start = ((bf16[8,2,128,128]{3,2,1,0:T(8,128)(2,1)}), bf16[8,2,128,128]{3,2,1,0:T(8,128)(2,1)S(1)}, u32[]{:S(2)}, u32[]{:S(2)}) async-start(bf16[8,2,128,128]{3,2,1,0:T(8,128)(2,1)} %pad_maximum_fusion.1.same0), calls=%async_computation | async-start | bytes 1048576 | tf_op jit(solution)/shard_map/all_to_all | solution.py:437
  44.1 12.6 %collective-permute-start.9 = (bf16[2,8,8192]{2,1,0:T(8,128)(2,1)}, bf16[2,8,8192]{2,1,0:T(8,128)(2,1)S(1)}, u32[]{:S(2)}, u32[]{:S(2)}) collective-permute-start(bf16[2,8,8192]{2,1,0:T(8,128)(2,1)} %get-tuple-element.119), channel_id=1, source_target_pairs={{97,32},{105,40},{113,48},{121,56},{101,36},{109,44},{117,52},{125... | collective-permute-start | bytes 786440 | tf_op jit(solution)/shard_map/ppermute | solution.py:400
  44.8 11.9 %collective-permute-start.10 = (bf16[2,8,8192]{2,1,0:T(8,128)(2,1)}, bf16[2,8,8192]{2,1,0:T(8,128)(2,1)S(1)}, u32[]{:S(2)}, u32[]{:S(2)}) collective-permute-start(bf16[2,8,8192]{2,1,0:T(8,128)(2,1)} %get-tuple-element.120), channel_id=1, source_target_pairs={{97,96},{105,104},{113,112},{121,120},{101,100},{109,108},{117,116... | collective-permute-start | bytes 786440 | tf_op jit(solution)/shard_map/ppermute | solution.py:400
  45.5 11.3 %collective-permute-start.11 = (bf16[2,8,8192]{2,1,0:T(8,128)(2,1)}, bf16[2,8,8192]{2,1,0:T(8,128)(2,1)S(1)}, u32[]{:S(2)}, u32[]{:S(2)}) collective-permute-start(bf16[2,8,8192]{2,1,0:T(8,128)(2,1)} %get-tuple-element.121), channel_id=1, source_target_pairs={{97,33},{105,41},{113,49},{121,57},{101,37},{109,45},{117,53},{125... | collective-permute-start | bytes 786440 | tf_op jit(solution)/shard_map/ppermute | solution.py:400
  57.7 37.7 %all-to-all-start.1 = ((bf16[8,2,8,1024]{3,2,1,0:T(8,128)(2,1)}), bf16[8,2,8,1024]{3,2,1,0:T(8,128)(2,1)S(1)}, u32[]{:S(2)}, u32[]{:S(2)}) async-start(bf16[8,2,8,1024]{3,2,1,0:T(8,128)(2,1)} %shard_map.86), calls=%async_computation.1 | async-start | bytes 524288 | tf_op jit(solution)/shard_map/all_to_all | solution.py:437
  67.2 47.0 %collective-permute-start.14 = (bf16[8,2,128,128]{3,2,1,0:T(8,128)(2,1)S(1)}, bf16[8,2,128,128]{3,2,1,0:T(8,128)(2,1)S(1)}, u32[]{:S(2)}, u32[]{:S(2)}) collective-permute-start(bf16[8,2,128,128]{3,2,1,0:T(8,128)(2,1)S(1)} %all-to-all-done), channel_id=1, source_target_pairs={{0,6},{8,14},{16,22},{24,30},{32,38},{40,46},{48,54},{56,62},{64,7... | collective-permute-start | bytes 1572872 | tf_op jit(solution)/shard_map/ppermute | solution.py:400
  84.3 29.9 %collective-permute-start.13 = (bf16[8,2,128,128]{3,2,1,0:T(8,128)(2,1)S(1)}, bf16[8,2,128,128]{3,2,1,0:T(8,128)(2,1)S(1)}, u32[]{:S(2)}, u32[]{:S(2)}) collective-permute-start(bf16[8,2,128,128]{3,2,1,0:T(8,128)(2,1)S(1)} %all-to-all-done), channel_id=1, source_target_pairs={{0,4},{8,12},{16,20},{24,28},{32,36},{40,44},{48,52},{56,60},{64,6... | collective-permute-start | bytes 1572872 | tf_op jit(solution)/shard_map/ppermute | solution.py:400
  84.3 29.9 %collective-permute-start.12 = (bf16[8,2,128,128]{3,2,1,0:T(8,128)(2,1)S(1)}, bf16[8,2,128,128]{3,2,1,0:T(8,128)(2,1)S(1)}, u32[]{:S(2)}, u32[]{:S(2)}) collective-permute-start(bf16[8,2,128,128]{3,2,1,0:T(8,128)(2,1)S(1)} %all-to-all-done), channel_id=1, source_target_pairs={{0,2},{8,10},{16,18},{24,26},{32,34},{40,42},{48,50},{56,58},{64,6... | collective-permute-start | bytes 1572872 | tf_op jit(solution)/shard_map/ppermute | solution.py:400
  96.3 19.8 %all-to-all-start.2 = ((bf16[16,2,8,1024]{3,2,1,0:T(8,128)(2,1)}), bf16[16,2,8,1024]{3,2,1,0:T(8,128)(2,1)S(1)}, u32[]{:S(2)}, u32[]{:S(2)}) async-start(bf16[16,2,8,1024]{3,2,1,0:T(8,128)(2,1)} %bitcast.7), calls=%async_computation.2 | async-start | bytes 1048576 | tf_op jit(solution)/shard_map/all_to_all | solution.py:437
  135.6 14.4 %all-to-all-start.3 = ((f32[4,24,256]{2,1,0:T(8,128)}), f32[4,24,256]{2,1,0:T(8,128)S(1)}, u32[]{:S(2)}, u32[]{:S(2)}) async-start(f32[4,24,256]{2,1,0:T(8,128)} %broadcast_in_dim.7), calls=%async_computation.3 | async-start | bytes 196608 | tf_op jit(solution)/shard_map/all_to_all | solution.py:437
  171.4 16.0 %all-to-all-start.4 = ((bf16[16,2,8,1024]{3,2,1,0:T(8,128)(2,1)}), bf16[16,2,8,1024]{3,2,1,0:T(8,128)(2,1)S(1)}, u32[]{:S(2)}, u32[]{:S(2)}) async-start(bf16[16,2,8,1024]{3,2,1,0:T(8,128)(2,1)} %get-tuple-element.205), calls=%async_computation.4 | async-start | bytes 1048576 | tf_op jit(solution)/shard_map/all_to_all | solution.py:437
  178.2 17.8 %collective-permute-start.23 = (bf16[8,2,128,128]{3,2,1,0:T(8,128)(2,1)S(1)}, bf16[8,2,128,128]{3,2,1,0:T(8,128)(2,1)}, u32[]{:S(2)}, u32[]{:S(2)}) collective-permute-start(bf16[8,2,128,128]{3,2,1,0:T(8,128)(2,1)S(1)} %copy-done.9), channel_id=1, source_target_pairs={{0,8},{8,0},{16,24},{24,16},{32,40},{40,32},{48,56},{56,48},{64,72... | collective-permute-start | bytes 1572872 | tf_op jit(solution)/shard_map/ppermute | solution.py:400
  180.4 29.9 %collective-permute-start.22 = (bf16[8,2,128,128]{3,2,1,0:T(8,128)(2,1)S(1)}, bf16[8,2,128,128]{3,2,1,0:T(8,128)(2,1)}, u32[]{:S(2)}, u32[]{:S(2)}) collective-permute-start(bf16[8,2,128,128]{3,2,1,0:T(8,128)(2,1)S(1)} %copy-done.8), channel_id=1, source_target_pairs={{0,8},{8,0},{16,24},{24,16},{32,40},{40,32},{48,56},{56,48},{64,72... | collective-permute-start | bytes 1572872 | tf_op jit(solution)/shard_map/ppermute | solution.py:400
  188.2 14.3 %all-to-all-start.5 = ((bf16[8,2,8,1024]{3,2,1,0:T(8,128)(2,1)}), bf16[8,2,8,1024]{3,2,1,0:T(8,128)(2,1)S(1)}, u32[]{:S(2)}, u32[]{:S(2)}) async-start(bf16[8,2,8,1024]{3,2,1,0:T(8,128)(2,1)} %concatenate.7), calls=%async_computation.5 | async-start | bytes 524288 | tf_op jit(solution)/shard_map/all_to_all | solution.py:437
  198.2 15.3 %collective-permute-start.24 = (bf16[8,2,128,128]{3,2,1,0:T(8,128)(2,1)}, bf16[8,2,128,128]{3,2,1,0:T(8,128)(2,1)S(1)}, u32[]{:S(2)}, u32[]{:S(2)}) collective-permute-start(bf16[8,2,128,128]{3,2,1,0:T(8,128)(2,1)} %add_convert_fusion.2), channel_id=1, source_target_pairs={{16,0},{24,8},{32,16},{40,24},{48,32},{56,40},{64,48},{72,56},{80,... | collective-permute-start | bytes 1572872 | tf_op jit(solution)/shard_map/ppermute | solution.py:400
  204.9 13.7 %collective-permute-start.28 = (bf16[8,2,128,128]{3,2,1,0:T(8,128)(2,1)S(1)}, bf16[8,2,128,128]{3,2,1,0:T(8,128)(2,1)S(1)}, u32[]{:S(2)}, u32[]{:S(2)}) collective-permute-start(bf16[8,2,128,128]{3,2,1,0:T(8,128)(2,1)S(1)} %get-tuple-element.231), channel_id=1, source_target_pairs={{0,2},{8,10},{16,18},{24,26},{32,34},{40,42},{48,50},{56,58},{64,6... | collective-permute-start | bytes 1572872 | tf_op jit(solution)/shard_map/ppermute | solution.py:400
  206.4 24.3 %collective-permute-start.27 = (bf16[8,2,128,128]{3,2,1,0:T(8,128)(2,1)S(1)}, bf16[8,2,128,128]{3,2,1,0:T(8,128)(2,1)S(1)}, u32[]{:S(2)}, u32[]{:S(2)}) collective-permute-start(bf16[8,2,128,128]{3,2,1,0:T(8,128)(2,1)S(1)} %get-tuple-element.232), channel_id=1, source_target_pairs={{0,4},{8,12},{16,20},{24,28},{32,36},{40,44},{48,52},{56,60},{64,6... | collective-permute-start | bytes 1572872 | tf_op jit(solution)/shard_map/ppermute | solution.py:400
  207.7 30.7 %collective-permute-start.26 = (bf16[8,2,128,128]{3,2,1,0:T(8,128)(2,1)S(1)}, bf16[8,2,128,128]{3,2,1,0:T(8,128)(2,1)S(1)}, u32[]{:S(2)}, u32[]{:S(2)}) collective-permute-start(bf16[8,2,128,128]{3,2,1,0:T(8,128)(2,1)S(1)} %get-tuple-element.230), channel_id=1, source_target_pairs={{0,6},{8,14},{16,22},{24,30},{32,38},{40,46},{48,54},{56,62},{64,7... | collective-permute-start | bytes 1572872 | tf_op jit(solution)/shard_map/ppermute | solution.py:400
  210.3 50.7 %collective-permute-start.18 = (bf16[4,2,8,8192]{3,2,1,0:T(8,128)(2,1)}, bf16[4,2,8,8192]{3,2,1,0:T(8,128)(2,1)}, u32[]{:S(2)}, u32[]{:S(2)}) collective-permute-start(bf16[4,2,8,8192]{3,2,1,0:T(8,128)(2,1)} %maximum_select_fusion), channel_id=1, source_target_pairs={{97,103},{105,111},{113,119},{121,127}} | collective-permute-start | bytes 3145736 | tf_op jit(solution)/shard_map/ppermute | solution.py:400
  213.5 47.5 %collective-permute-start.19 = (bf16[4,2,8,8192]{3,2,1,0:T(8,128)(2,1)}, bf16[4,2,8,8192]{3,2,1,0:T(8,128)(2,1)}, u32[]{:S(2)}, u32[]{:S(2)}) collective-permute-start(bf16[4,2,8,8192]{3,2,1,0:T(8,128)(2,1)} %maximum_select_fusion), channel_id=1, source_target_pairs={{101,103},{109,111},{117,119},{125,127}} | collective-permute-start | bytes 3145736 | tf_op jit(solution)/shard_map/ppermute | solution.py:400
  218.6 42.4 %collective-permute-start.20 = (bf16[4,2,8,8192]{3,2,1,0:T(8,128)(2,1)}, bf16[4,2,8,8192]{3,2,1,0:T(8,128)(2,1)}, u32[]{:S(2)}, u32[]{:S(2)}) collective-permute-start(bf16[4,2,8,8192]{3,2,1,0:T(8,128)(2,1)} %maximum_select_fusion), channel_id=1, source_target_pairs={{38,103},{46,111},{54,119},{62,127}} | collective-permute-start | bytes 3145736 | tf_op jit(solution)/shard_map/ppermute | solution.py:400
  230.6 30.4 %collective-permute-start.21 = (bf16[4,2,8,8192]{3,2,1,0:T(8,128)(2,1)}, bf16[4,2,8,8192]{3,2,1,0:T(8,128)(2,1)}, u32[]{:S(2)}, u32[]{:S(2)}) collective-permute-start(bf16[4,2,8,8192]{3,2,1,0:T(8,128)(2,1)} %maximum_select_fusion), channel_id=1, source_target_pairs={{39,103},{47,111},{55,119},{63,127}} | collective-permute-start | bytes 3145736 | tf_op jit(solution)/shard_map/ppermute | solution.py:400
  238.4 15.3 %collective-permute-start.25 = (bf16[8,2,128,128]{3,2,1,0:T(8,128)(2,1)}, bf16[8,2,128,128]{3,2,1,0:T(8,128)(2,1)}, u32[]{:S(2)}, u32[]{:S(2)}) collective-permute-start(bf16[8,2,128,128]{3,2,1,0:T(8,128)(2,1)} %add_convert_fusion.1), channel_id=1, source_target_pairs={{16,0},{24,8},{32,16},{40,24},{48,32},{56,40},{64,48},{72,56},{80,... | collective-permute-start | bytes 1572872 | tf_op jit(solution)/shard_map/ppermute | solution.py:400
  240.8 16.7 %all-to-all-start.6 = ((bf16[8,2,128,128]{3,2,1,0:T(8,128)(2,1)}), bf16[8,2,128,128]{3,2,1,0:T(8,128)(2,1)S(1)}, u32[]{:S(2)}, u32[]{:S(2)}) async-start(bf16[8,2,128,128]{3,2,1,0:T(8,128)(2,1)} %fusion.2), calls=%async_computation.6 | async-start | bytes 1048576 | tf_op jit(solution)/shard_map/all_to_all | solution.py:437
  (20 other events, 252.2 us)
